TPU v7x, 128 devices: a whole 4x4x4 slice. The times are simulated.
128 devices in a mesh: front: 8 (over z, core), grid: 16 (over y, x).
Axes of the slice: x: 4, y: 4, z: 4, core: 2. Of those that a mesh axis runs over, the one named last changes fastest.
Arguments:
- pivot_block: float32 [8, 512, 512], P('front'), as said below
- border: float32 [8, 8192, 512], P('front', 'grid'), may hold values from -0.9 to 0.9
- trailing: float32 [8, 8192, 8192], P('front', 'grid'), as said below
- dest_owner: int32 [8, 2560, 1], P('front', 'grid'), may hold values from 0 to 127; in each aligned block of 160 rows (0 to 159, 160 to 319, ..., all dimensions but the last counted through in order) at most 2 rows name the same one
- dest_slot: int32 [8, 2560], P('front', 'grid'), may hold values from 0 to 63
- row_map: int32 [8, 2560, 128], P('front', 'grid'), may hold values from 0 to 127, each once within a row
Outputs:
- pivot_factor: float32 [8, 512, 512], P('front')
- border_factor: float32 [8, 8192, 512], P('front', 'grid')
- ancestor_blocks: float32 [8192, 128, 128], P(('front', 'grid'))
Inputs may be any that keep to these rules, and one draw needn't show every extreme that they name: `pivot_block`: symmetric positive definite. `trailing`: Symmetric. `dest_owner`: in each aligned block of 160 entries no owner is named more than 2 times, a bound that some block reaches.
All inputs are finite; a program needn't handle non-finite values.
Results may differ from a plain program's by a relative error of at most 0.0001.
Values sent between devices are 32-bit elements; how exact they have to be, the bound alone decides.
A program may use at most 192 MiB of HBM per device.

v0:
```python
import jax
import jax.numpy as jnp
from jax import lax
from jax.sharding import PartitionSpec as P

BLK = 128
NB = 256
SLOTS = 64


precise = lax.Precision.HIGHEST


def factor_panels(corner, border_rows_in):
    first_factor = jnp.linalg.cholesky(corner[:NB, :NB])
    remainder = jnp.concatenate([corner[NB:, :NB], border_rows_in[:, :NB]], axis=0)
    solved = jax.scipy.linalg.solve_triangular(first_factor, remainder.T, lower=True).T
    pivot_rows = solved[:NB]
    border_rows = solved[NB:]
    updated_pivot = corner[NB:, NB:] - jnp.dot(pivot_rows, pivot_rows.T, precision=precise)
    updated_border = border_rows_in[:, NB:] - jnp.dot(border_rows, pivot_rows.T, precision=precise)
    second_factor = jnp.linalg.cholesky(updated_pivot)
    second_border = jax.scipy.linalg.solve_triangular(second_factor, updated_border.T, lower=True).T
    upper_half = jnp.concatenate([first_factor, jnp.zeros((NB, NB), jnp.float32)], axis=1)
    lower_half = jnp.concatenate([pivot_rows, second_factor], axis=1)
    return (
        jnp.concatenate([upper_half, lower_half], axis=0),
        jnp.concatenate([border_rows, second_border], axis=1),
    )


def subtract_outer(base_rows, left_rows, piece):
    return base_rows - jnp.einsum("rk,ck->rc", left_rows, piece, precision=precise)


def body(pivot_block, border, trailing, dest_owner, dest_slot, row_map):
    pivot_factor, border_factor = factor_panels(pivot_block[0], border[0])
    local_rows = trailing[0]
    schur_rows = local_rows
    for column_start in (0, NB):
        panel_cols = border_factor[:, column_start : column_start + NB]
        schur_rows = subtract_outer(
            schur_rows, panel_cols, lax.all_gather(panel_cols, "grid", axis=0, tiled=True)
        )
    group_size = lax.axis_size("grid")
    member = lax.axis_index("grid")
    per_dev = local_rows.shape[0] // BLK
    blocks_all = local_rows.shape[1] // BLK
    listed = dest_owner.shape[1]
    candidates = jnp.arange(per_dev * blocks_all, dtype=jnp.int32)
    local_block = candidates // blocks_all
    column_block = candidates % blocks_all
    true_column = column_block % per_dev * group_size + column_block // per_dev
    true_row = local_block * group_size + member
    usable = true_column <= true_row
    position = jnp.cumsum(usable.astype(jnp.int32)) - 1
    matches = (
        usable[None, :] & (position[None, :] == jnp.arange(listed, dtype=jnp.int32)[:, None])
    ).astype(jnp.float32)
    front_count = lax.axis_size("front")
    devices = front_count * group_size
    capacity = max(2, (listed + devices - 1) // devices)
    owner_id = dest_owner[0, :, 0]
    owner_hits = (owner_id[:, None] == jnp.arange(devices, dtype=jnp.int32)[None, :]).astype(
        jnp.int32
    )
    earlier = jnp.cumsum(owner_hits, axis=0) - owner_hits
    rank_in = jnp.sum(earlier * owner_hits, axis=1)
    buffer_place = owner_id * capacity + rank_in
    slot_hits = buffer_place[None, :] == jnp.arange(devices * capacity, dtype=jnp.int32)[:, None]
    sender = jnp.sum(
        slot_hits.astype(jnp.int32) * jnp.arange(listed, dtype=jnp.int32)[None, :], axis=1
    )
    filled = jnp.any(slot_hits, axis=1)
    selector = jnp.dot(slot_hits.astype(jnp.float32), matches, precision=precise)
    selector = selector.reshape(devices * capacity, per_dev, blocks_all)
    blocked = schur_rows.reshape(per_dev, BLK, blocks_all, BLK)
    picked = jnp.einsum("qkc,krcs->qrs", selector, blocked, precision=precise)
    row_order = row_map[0][sender]
    permuter = (row_order[:, :, None] == jnp.arange(BLK, dtype=jnp.int32)[None, None, :]).astype(
        jnp.float32
    )
    moved = jnp.einsum("qrs,qsx->qrx", permuter, picked, precision=precise)
    outgoing = moved.reshape(devices, capacity, BLK * BLK)
    slot_out = jnp.where(filled, dest_slot[0][sender], 0).reshape(devices, capacity)
    arrived, slot_in = (
        lax.all_to_all(outgoing, ("front", "grid"), split_axis=0, concat_axis=0, tiled=True),
        lax.all_to_all(slot_out, ("front", "grid"), split_axis=0, concat_axis=0, tiled=True),
    )
    arrived = arrived.reshape(devices * capacity, BLK * BLK)
    slot_in = slot_in.reshape(devices * capacity)
    chooser = (slot_in[:, None] == jnp.arange(SLOTS, dtype=jnp.int32)[None, :]).astype(jnp.float32)
    summed = jnp.einsum("rs,rx->sx", chooser, arrived, precision=precise)
    return (pivot_factor[None], border_factor[None], summed.reshape(SLOTS, BLK, BLK))


def solution(mesh):
    return jax.shard_map(
        body,
        mesh=mesh,
        in_specs=(
            P("front", None, None),
            P("front", "grid", None),
            P("front", "grid", None),
            P("front", "grid", None),
            P("front", "grid"),
            P("front", "grid", None),
        ),
        out_specs=(
            P("front", None, None),
            P("front", "grid", None),
            P(("front", "grid"), None, None),
        ),
        check_vma=False,
    )
```

profile of v0, /device:TPU:5, one launch (start us, length us, event | category | flops | bytes accessed | tf_op | source)
XLA Modules:
  0.0 670.3 jit_solution(7392036229213009177)
XLA Ops:
  7.3 1.6 copy.53
  9.1 11.7 %cholesky.130 = f32[128,128]{1,0:T(8,128)S(1)} custom-call(f32[128,128]{1,0:T(8,128)S(1)} %cholesky.194), custom_call_target="Cholesky" | custom-call | tf_op jit(solution)/shard_map/jit(cholesky)/cholesky | solution.py:15
  20.8 9.8 %custom-call.19 = f32[1,128,128]{1,2,0:T(8,128)S(1)} custom-call(f32[1,128,128]{2,1,0:T(8,128)S(1)} %get-tuple-element.65), custom_call_target="InvertDiagBlocksLowerTriangular" | custom-call | tf_op jit(solution)/shard_map/jit(cholesky)/cholesky | solution.py:15
  31.1 11.7 %cholesky.147 = f32[128,128]{1,0:T(8,128)S(1)} custom-call(f32[128,128]{1,0:T(8,128)S(1)} %convolution_subtract_fusion.5), custom_call_target="Cholesky" | custom-call | tf_op jit(solution)/shard_map/jit(cholesky)/cholesky | solution.py:15
  45.7 4.3 while.2
  46.5 1.4 bitcast_dynamic-update-slice_fusion.4
  48.5 1.4 bitcast_dynamic-update-slice_fusion.4
  49.9 19.7 %custom-call.16 = f32[2,128,128]{1,2,0:T(8,128)S(1)} custom-call(f32[2,128,128]{2,1,0:T(8,128)S(1)} %get-tuple-element.11), custom_call_target="InvertDiagBlocksLowerTriangular" | custom-call | tf_op jit(solution)/shard_map/jit(_solve_triangular)/triangular_solve | solution.py:17
  69.6 1.6 copy.55
  76.6 11.7 %cholesky.164 = f32[128,128]{1,0:T(8,128)S(1)} custom-call(f32[128,128]{1,0:T(8,128)S(1)} %cholesky.197), custom_call_target="Cholesky" | custom-call | tf_op jit(solution)/shard_map/jit(cholesky)/cholesky | solution.py:22
  88.4 9.8 %custom-call.20 = f32[1,128,128]{1,2,0:T(8,128)S(1)} custom-call(f32[1,128,128]{2,1,0:T(8,128)S(1)} %get-tuple-element.61), custom_call_target="InvertDiagBlocksLowerTriangular" | custom-call | tf_op jit(solution)/shard_map/jit(cholesky)/cholesky | solution.py:22
  98.9 11.7 %cholesky.181 = f32[128,128]{1,0:T(8,128)S(1)} custom-call(f32[128,128]{1,0:T(8,128)S(1)} %convolution_subtract_fusion.4), custom_call_target="Cholesky" | custom-call | tf_op jit(solution)/shard_map/jit(cholesky)/cholesky | solution.py:22
  113.2 12.1 %while.3 = (s32[]{:T(128)}, f32[256,256]{1,0:T(8,128)S(1)}, s32[2,2]{1,0:T(2,128)S(1)}, f32[2,128,128]{2,1,0:T(8,128)S(1)}, s32[]{:T(128)}) while((s32[]{:T(128)}, f32[256,256]{1,0:T(8,128)S(1)}, s32[2,2]{1,0:T(2,128)S(1)}, f32[2,128,128]{2,1,0:T(8,128)S(1)}, s32[]{:T(128)}) %tuple.61), condition=%wide.while_cond.1, body=%wide.while_body.1.sunk | while | flops 2 | bytes 131181 | solution.py:23
  122.1 1.3 bitcast_dynamic-update-slice_fusion.5
  124.0 1.3 bitcast_dynamic-update-slice_fusion.5
  125.3 19.7 %custom-call.17 = f32[2,128,128]{1,2,0:T(8,128)S(1)} custom-call(f32[2,128,128]{2,1,0:T(8,128)S(1)} %get-tuple-element.19), custom_call_target="InvertDiagBlocksLowerTriangular" | custom-call | tf_op jit(solution)/shard_map/jit(_solve_triangular)/triangular_solve | solution.py:23
  146.6 1.4 fusion.33
  149.6 1.9 gather_fusion
  152.4 10.8 %all-to-all-start = ((s32[128,1,2]{2,1,0:T(1,128)}), s32[128,1,2]{2,1,0:T(1,128)S(1)}, u32[]{:S(2)}, u32[]{:S(2)}) async-start(s32[128,1,2]{2,1,0:T(1,128)} %bitcast.26), calls=%async_computation | async-start | bytes 131072 | tf_op jit(solution)/shard_map/all_to_all | solution.py:88
  165.0 18.5 %fusion.56 = f32[512,8192]{1,0:T(8,128)} fusion(f32[8192,256]{1,0:T(8,128)} %all-gather.3.cloned.1.call-done, f32[768,256]{1,0:T(8,128)S(1)} %maximum_bitcast_fusion.2), kind=kOutput, calls=%fused_computation.134 | convolution fusion | flops 12884901888 | bytes 25690112 | tf_op jit(solution)/shard_map/rk,ck->rc/dot_general | solution.py:33
  183.5 39.6 %all-gather.5.cloned.1.call-done = f32[8192,256]{1,0:T(8,128)} async-done(((f32[512,256]{1,0:T(8,128)}), f32[8192,256]{1,0:T(8,128)}) %all-gather.5.cloned.1.call-update) | async-done | bytes 8388624 | tf_op jit(solution)/shard_map/all_gather | solution.py:43
  223.1 42.1 %fusion.3 = f32[64,8,64,128]{3,1,2,0:T(8,128)} fusion(f32[512,8192]{1,0:T(8,128)} %fusion.56, f32[1,512,8192]{2,1,0:T(8,128)} %param.9, f32[8192,256]{1,0:T(8,128)} %all-gather.5.cloned.1.call-done, f32[128,512]{0,1:T(8,128)S(1)} %fusion.33, f32[128,512]{0,1:T(8,128)S(1)} %copy.62), kind=kOutput, calls=%fused_computation.10 | convolution fusion | flops 12893421568 | bytes 59244544 | tf_op jit(solution)/shard_map/rk,ck->rc/dot_general | solution.py:33
  265.2 14.1 %copy.76 = f32[64,8,64,128]{3,2,1,0:T(8,128)} copy(f32[64,8,64,128]{3,1,2,0:T(8,128)} %fusion.3) | data formatting | bytes 33554432
  279.3 18.7 %fusion.6 = f32[256,128,128]{2,0,1:T(8,128)S(1)} fusion(f32[256,4,64,1]{0,2,3,1:T(8,128)S(1)} %bitcast.140, f32[4,128,64,128]{3,2,1,0:T(8,128)} %bitcast.130), kind=kOutput, calls=%fused_computation.14 | convolution fusion | flops 12884901888 | bytes 33816576 | tf_op jit(solution)/shard_map/qkc,krcs->qrs/dot_general | solution.py:78
  298.0 26.6 %fusion.4 = f32[256,128,128]{2,1,0:T(8,128)} fusion(f32[256,128,128]{2,0,1:T(8,128)S(1)} %fusion.6, s32[256,128]{1,0:T(8,128)S(1)} %gather_fusion.1), kind=kOutput, calls=%fused_computation.11 | convolution fusion | flops 6446645248 | bytes 33685504 | tf_op jit(solution)/shard_map/qrs,qsx->qrx/dot_general | solution.py:83
  324.6 19.8 %reshape.216 = f32[128,2,16384]{2,1,0:T(2,128)} reshape(f32[256,128,128]{2,1,0:T(8,128)} %fusion.4) | data formatting | bytes 33554432 | tf_op jit(solution)/shard_map/reshape | solution.py:84
  344.4 9.2 %all-to-all-start.1 = ((f32[128,2,16384]{2,1,0:T(2,128)}), f32[128,2,16384]{2,1,0:T(2,128)}, u32[]{:S(2)}, u32[]{:S(2)}) async-start(f32[128,2,16384]{2,1,0:T(2,128)} %reshape.216), calls=%async_computation.1 | async-start | bytes 33554432 | tf_op jit(solution)/shard_map/all_to_all | solution.py:87
  357.3 251.7 %all-to-all-done.1 = f32[128,2,16384]{2,1,0:T(2,128)} async-done(((f32[128,2,16384]{2,1,0:T(2,128)}), f32[128,2,16384]{2,1,0:T(2,128)}, u32[]{:S(2)}, u32[]{:S(2)}) %all-to-all-start.1) | async-done | bytes 16777248 | tf_op jit(solution)/shard_map/all_to_all | solution.py:87
  609.0 20.5 %reshape.217 = f32[256,16384]{1,0:T(8,128)} reshape(f32[128,2,16384]{2,1,0:T(2,128)} %all-to-all-done.1) | data formatting | bytes 33554432 | tf_op jit(solution)/shard_map/reshape | solution.py:90
  629.5 17.5 %copy.69 = f32[256,16384]{0,1:T(8,128)} copy(f32[256,16384]{1,0:T(8,128)} %reshape.217) | data formatting | bytes 33554432 | tf_op jit(solution)/shard_map/reshape | solution.py:90
  647.0 11.5 %fusion.43 = f32[64,128,128]{2,0,1:T(8,128)S(1)} fusion(f32[128,128,256]{2,1,0:T(8,128)} %bitcast.129, s32[256]{0:T(256)S(1)} %eq.86), kind=kOutput, calls=%fused_computation.86 | convolution fusion | flops 3221241856 | bytes 20972544 | tf_op jit(solution)/shard_map/rs,rx->sx/dot_general | solution.py:93
  658.5 4.4 copy.70
  (104 shorter events, 21.4 us)
Async XLA Ops:
  7.2 156.5 %copy-start = (s32[1,160,128]{2,1,0:T(8,128)S(1)}, s32[1,160,128]{2,1,0:T(8,128)}, u32[]{:S(2)}) copy-start(s32[1,160,128]{2,1,0:T(8,128)} %param.12) | copy-start | bytes 245764
  7.2 141.7 %copy-start.7 = (s32[1,160,1]{1,2,0:T(1,128)S(1)}, s32[1,160,1]{1,2,0:T(1,128)}, u32[]{:S(2)}) copy-start(s32[1,160,1]{1,2,0:T(1,128)} %param.10) | copy-start | bytes 1924
  7.2 142.4 %copy-start.2 = (s32[1,160]{1,0:T(1,128)S(1)}, s32[1,160]{1,0:T(1,128)}, u32[]{:S(2)}) copy-start(s32[1,160]{1,0:T(1,128)} %param.11) | copy-start | bytes 1924
  7.2 157.7 %all-gather.3.cloned.1.call-start = ((), (), s32[]{:S(2)}) async-start(), calls=%async_computation.2 | async-start | bytes 8912896 | tf_op jit(solution)/shard_map/all_gather | solution.py:43
  76.0 147.1 %all-gather.5.cloned.1.call-start = ((), (), s32[]{:S(2)}) async-start(), calls=%async_computation.3 | async-start | bytes 8912896 | tf_op jit(solution)/shard_map/all_gather | solution.py:43
  145.0 0.7 copy-start.6
  152.4 192.0 %all-to-all-start = ((s32[128,1,2]{2,1,0:T(1,128)}), s32[128,1,2]{2,1,0:T(1,128)S(1)}, u32[]{:S(2)}, u32[]{:S(2)}) async-start(s32[128,1,2]{2,1,0:T(1,128)} %bitcast.26), calls=%async_computation | async-start | bytes 131072 | tf_op jit(solution)/shard_map/all_to_all | solution.py:88
  344.4 9.2 %copy-start.3 = (f32[512,256]{1,0:T(8,128)S(1)}, f32[512,256]{1,0:T(8,128)}, u32[]{:S(2)}) copy-start(f32[512,256]{1,0:T(8,128)} %slice.133) | copy-start | bytes 1572868
  344.4 9.2 %copy-start.4 = (f32[512,256]{1,0:T(8,128)S(1)}, f32[512,256]{1,0:T(8,128)}, u32[]{:S(2)}) copy-start(f32[512,256]{1,0:T(8,128)} %fusion.12) | copy-start | bytes 1572868
  344.4 10.4 %copy-start.5 = (f32[256,256]{1,0:T(8,128)S(1)}, f32[256,256]{1,0:T(8,128)}, u32[]{:S(2)}) copy-start(f32[256,256]{1,0:T(8,128)} %get-tuple-element.51) | copy-start | bytes 786436
  344.4 264.6 %all-to-all-start.1 = ((f32[128,2,16384]{2,1,0:T(2,128)}), f32[128,2,16384]{2,1,0:T(2,128)}, u32[]{:S(2)}, u32[]{:S(2)}) async-start(f32[128,2,16384]{2,1,0:T(2,128)} %reshape.216), calls=%async_computation.1 | async-start | bytes 33554432 | tf_op jit(solution)/shard_map/all_to_all | solution.py:87
  629.5 33.5 %copy-start.1 = (s32[1,160,128]{2,1,0:T(8,128)S(1)}, s32[1,160,128]{2,1,0:T(8,128)}, u32[]{:S(2)}) copy-start(s32[1,160,128]{2,1,0:T(8,128)} %param.12) | copy-start | bytes 245764
Sparse Core Ops, SparseCore 0:
  76.1 73.0 all-gather.2
  151.9 71.1 all-gather.4
where the time goes:
time: 680 us; the launch traced here: 670 us
  waiting for transfers between devices  291 us (43%)
  matrix products  124 us (18%)
  other arithmetic  115 us (17%)
  local copies, waits for them, and re-layouts  94 us (14%)
  starting transfers between devices  20.1 us (3%)
  between operations  17.6 us (3%)
  loops' own time  8.6 us (1%)
    all_to_all x1, waiting for transfers between devices, body(): lax.all_to_all(outgoing, ('front', 'grid'), split_axis=0, concat_axis=0,...  252 us
    dot_general x2, matrix products, subtract_outer(): jnp.einsum('rk,ck->rc', left_rows, piece, precision=precise)  60.6 us
    all_gather x2, waiting for transfers between devices, body(): lax.all_gather(panel_cols, 'grid', axis=0, tiled=True)  39.6 us
    reshape x2, local copies, waits for them, and re-layouts, body(): arrived = arrived.reshape(devices * capacity, BLK * BLK)  38 us
    another operation x7, other arithmetic, factor_panels(): second_factor = jnp.linalg.cholesky(updated_pivot)  34.6 us
    another operation x6, other arithmetic, factor_panels(): first_factor = jnp.linalg.cholesky(corner[:NB, :NB])  34 us
    dot_general x1, matrix products, body(): moved = jnp.einsum('qrs,qsx->qrx', permuter, picked, precision=precise)  26.6 us
    unnamed x23, local copies, waits for them, and re-layouts  21.7 us
  transfers between devices with their start and end apart: 4, of which 2 were waited for; matrix products, arithmetic and copies ran while one was open for 32% of the time, Pallas kernels for 0%

commit v1 on v0

v1 whole, which is shorter than its diff:
```python
import functools

import jax
import jax.numpy as jnp
import numpy as np
from jax import lax
from jax.experimental import pallas as pl
from jax.experimental.pallas import tpu as pltpu
from jax.sharding import PartitionSpec as P

BLK = 128
SLOTS = 64
N_GRID = 16
GROUP = 4
P_SIZE = 512
HI = lax.Precision.HIGHEST
VMEM = pl.BlockSpec(memory_space=pltpu.VMEM)


def tdot(a, b):
    return lax.dot_general(a, b, (((0,), (0,)), ((), ())), precision=HI, preferred_element_type=jnp.float32)


def factor_diagonal(block):
    aug = jnp.concatenate([block, jnp.eye(BLK, dtype=jnp.float32)], axis=1)
    sub = lax.broadcasted_iota(jnp.int32, (8, BLK), 0)
    sub2 = lax.broadcasted_iota(jnp.int32, (8, 2 * BLK), 0)
    done = []
    for panel in range(BLK // 8):
        rows = aug[:8]
        cols = [jnp.broadcast_to(rows[:, 8 * panel + m : 8 * panel + m + 1], (8, BLK)) for m in range(8)]
        for i in range(8):
            inv = lax.rsqrt(jnp.broadcast_to(cols[i][i : i + 1], (8, BLK)))
            mult = jnp.where(sub > i, cols[i] * inv, 0.0)
            inv2 = jnp.concatenate([inv, inv], axis=1)
            mult2 = jnp.concatenate([mult, mult], axis=1)
            top = jnp.broadcast_to(rows[i : i + 1], (8, 2 * BLK)) * inv2
            rows = jnp.where(sub2 == i, top, rows - mult2 * top)
            for m in range(i + 1, 8):
                cols[m] = cols[m] - mult * (jnp.broadcast_to(cols[m][i : i + 1], (8, BLK)) * inv)
        done.append(rows)
        if panel < BLK // 8 - 1:
            left = rows[:, :BLK]
            update = tdot(left, rows)
            aug = aug[8:] - update[8 * (panel + 1) :]
    full = jnp.concatenate(done, axis=0)
    r = lax.broadcasted_iota(jnp.int32, (BLK, BLK), 0)
    c = lax.broadcasted_iota(jnp.int32, (BLK, BLK), 1)
    return jnp.where(r <= c, full[:, :BLK], 0.0), full[:, BLK:]


def factor_kernel(a_ref, b_ref, pivot_ref, border_ref, whi_ref, wlo_ref, aug_ref):
    r = lax.broadcasted_iota(jnp.int32, (P_SIZE, P_SIZE), 0)
    c = lax.broadcasted_iota(jnp.int32, (P_SIZE, P_SIZE), 1)
    aug_ref[:, :P_SIZE] = a_ref[...]
    aug_ref[:, P_SIZE:] = jnp.where(r == c, 1.0, 0.0)
    lane = lax.broadcasted_iota(jnp.int32, (BLK, 2 * P_SIZE), 1)

    def step(b, _):
        start = pl.multiple_of(b * BLK, BLK)
        stripe = aug_ref[pl.ds(start, BLK), :]
        diag = aug_ref[pl.ds(start, BLK), pl.ds(start, BLK)]
        upper, inverse = factor_diagonal(diag)
        solved = jnp.dot(inverse, stripe, precision=HI, preferred_element_type=jnp.float32)
        solved = jnp.where(lane >= start, solved, 0.0)
        aug_ref[pl.ds(start, BLK), :] = solved
        aug_ref[pl.ds(start, BLK), pl.ds(start, BLK)] = upper

        def rest(k, _):
            at = pl.multiple_of(k * BLK, BLK)
            left = aug_ref[pl.ds(start, BLK), pl.ds(at, BLK)]
            aug_ref[pl.ds(at, BLK), :] = aug_ref[pl.ds(at, BLK), :] - tdot(left, aug_ref[pl.ds(start, BLK), :])
            return 0

        lax.fori_loop(b + 1, P_SIZE // BLK, rest, 0)
        return 0

    lax.fori_loop(0, P_SIZE // BLK, step, 0)
    pivot_ref[...] = jnp.where(r >= c, aug_ref[:, :P_SIZE].T, 0.0)
    inverse = jnp.where(r >= c, aug_ref[:, P_SIZE:], 0.0)
    solved = lax.dot_general(b_ref[...], inverse, (((1,), (1,)), ((), ())), precision=HI, preferred_element_type=jnp.float32)
    border_ref[...] = solved
    weights = jnp.dot(solved, inverse, precision=HI, preferred_element_type=jnp.float32)
    high = weights.astype(jnp.bfloat16)
    whi_ref[...] = high
    wlo_ref[...] = (weights - high.astype(jnp.float32)).astype(jnp.bfloat16)


def factor(a, b):
    sq = jax.ShapeDtypeStruct((P_SIZE, P_SIZE), jnp.float32)
    half = jax.ShapeDtypeStruct((P_SIZE, P_SIZE), jnp.bfloat16)
    return pl.pallas_call(
        factor_kernel,
        out_shape=(sq, sq, half, half),
        in_specs=[VMEM, VMEM],
        out_specs=(VMEM, VMEM, VMEM, VMEM),
        scratch_shapes=[pltpu.VMEM((P_SIZE, 2 * P_SIZE), jnp.float32)],
        compiler_params=pltpu.CompilerParams(vmem_limit_bytes=32 << 20),
        name="factor",
    )(a, b)


def tile_table():
    per_dev = 8192 // (N_GRID * BLK)
    table = np.full((N_GRID, 160), -1, np.int32)
    for member in range(N_GRID):
        place = 0
        for local in range(per_dev):
            for column in range(8192 // BLK):
                if column % per_dev * N_GRID + column // per_dev <= local * N_GRID + member:
                    table[member, place] = local * (8192 // BLK) + column
                    place += 1
    return table


def tiles_kernel(tile_ref, entry_ref, whi_ref, wlo_ref, map_ref, *refs):
    trailing = refs[:GROUP]
    border = refs[GROUP : 2 * GROUP]
    out_ref = refs[2 * GROUP]
    step = pl.program_id(0)
    for t in range(GROUP):
        tile = tile_ref[step * GROUP + t]
        entry = entry_ref[step * GROUP + t]

        @pl.when(tile >= 0)
        def _(t=t, tile=tile, entry=entry):
            at = pl.multiple_of(tile // 64 * BLK, BLK)
            cols = border[t][...]
            high = cols.astype(jnp.bfloat16)
            low = (cols - high.astype(jnp.float32)).astype(jnp.bfloat16)
            left_high = whi_ref[pl.ds(at, BLK), :]
            left = jnp.concatenate([left_high, left_high, wlo_ref[pl.ds(at, BLK), :]], axis=1)
            right = jnp.concatenate([high, low, high], axis=1)
            product = lax.dot_general(left, right, (((1,), (1,)), ((), ())), preferred_element_type=jnp.float32)
            value = trailing[t][...] - product
            upper = value.astype(jnp.bfloat16)
            lower = (value - upper.astype(jnp.float32)).astype(jnp.bfloat16)
            source = jnp.broadcast_to(map_ref[pl.ds(entry, 1), :], (BLK, BLK))
            chosen = source == lax.broadcasted_iota(jnp.int32, (BLK, BLK), 0)
            chosen = jnp.where(chosen, 1.0, 0.0).astype(jnp.bfloat16)
            moved = lax.dot_general(chosen, jnp.concatenate([upper, lower], axis=1), (((0,), (0,)), ((), ())), preferred_element_type=jnp.float32)
            out_ref[t] = moved[:, :BLK] + moved[:, BLK:]


def tiles(tile, entry, whi, wlo, row_map, trailing, border_all):
    def trailing_map(t):
        def index(i, tile_ref, entry_ref):
            at = jnp.maximum(tile_ref[i * GROUP + t], 0)
            return at // 64, at % 64
        return index

    def border_map(t):
        def index(i, tile_ref, entry_ref):
            return jnp.maximum(tile_ref[i * GROUP + t], 0) % 64, 0
        return index

    def whole(i, tile_ref, entry_ref):
        return 0, 0

    count = tile.shape[0]
    return pl.pallas_call(
        tiles_kernel,
        out_shape=jax.ShapeDtypeStruct((count, BLK, BLK), jnp.float32),
        grid_spec=pltpu.PrefetchScalarGridSpec(
            num_scalar_prefetch=2,
            grid=(count // GROUP,),
            in_specs=[
                pl.BlockSpec((P_SIZE, P_SIZE), whole),
                pl.BlockSpec((P_SIZE, P_SIZE), whole),
                pl.BlockSpec((160, BLK), whole),
            ]
            + [pl.BlockSpec((BLK, BLK), trailing_map(t)) for t in range(GROUP)]
            + [pl.BlockSpec((BLK, P_SIZE), border_map(t)) for t in range(GROUP)],
            out_specs=pl.BlockSpec((GROUP, BLK, BLK), lambda i, tile_ref, entry_ref: (i, 0, 0)),
        ),
        compiler_params=pltpu.CompilerParams(vmem_limit_bytes=40 << 20),
        cost_estimate=pl.CostEstimate(flops=count * 2 * BLK * BLK * 1792, transcendentals=0, bytes_accessed=count * 384 * 1024),
        name="tiles",
    )(tile, entry, whi, wlo, row_map, *([trailing] * GROUP), *([border_all] * GROUP))


def sum_kernel(first, slot_ref, *refs):
    arrived_ref, out_ref = refs[-2:]
    step = pl.program_id(0)

    @pl.when(step == 0)
    def _():
        out_ref[...] = jnp.zeros_like(out_ref) if first else refs[0][...]

    for t in range(8):
        slot = slot_ref[step * 8 + t]

        @pl.when(slot >= 0)
        def _(t=t, slot=slot):
            out_ref[slot] = out_ref[slot] + arrived_ref[t]


def slot_sums(slot, arrived, before=None):
    count = arrived.shape[0]
    whole = pl.BlockSpec((SLOTS, BLK, BLK), lambda i, slot_ref: (0, 0, 0))
    first = before is None
    return pl.pallas_call(
        functools.partial(sum_kernel, first),
        out_shape=jax.ShapeDtypeStruct((SLOTS, BLK, BLK), jnp.float32),
        grid_spec=pltpu.PrefetchScalarGridSpec(
            num_scalar_prefetch=1,
            grid=(count // 8,),
            in_specs=([] if first else [whole]) + [pl.BlockSpec((8, BLK, BLK), lambda i, slot_ref: (i, 0, 0))],
            out_specs=whole,
        ),
        compiler_params=pltpu.CompilerParams(vmem_limit_bytes=40 << 20),
        cost_estimate=pl.CostEstimate(flops=count * BLK * BLK, transcendentals=0, bytes_accessed=count * 64 * 1024),
        name="slot_sums",
    )(slot, *([] if first else [before]), arrived)


def body(pivot_block, border, trailing, dest_owner, dest_slot, row_map):
    border_all = lax.all_gather(border[0], "grid", axis=0, tiled=True)
    pivot_factor, border_factor, whi, wlo = factor(pivot_block[0], border[0])
    member = lax.axis_index("grid")
    devices = lax.axis_size("front") * lax.axis_size("grid")
    listed = dest_owner.shape[1]
    table = jnp.asarray(tile_table())[member]
    owner = dest_owner[0, :, 0]
    hits = (owner[:, None] == jnp.arange(devices, dtype=jnp.int32)[None, :]) & (table >= 0)[:, None]
    counted = hits.astype(jnp.int32)
    before = jnp.arange(listed)[:, None] > jnp.arange(listed)[None, :]
    later = jnp.dot(before.astype(jnp.bfloat16), counted.astype(jnp.bfloat16), preferred_element_type=jnp.float32) > 0.5
    entries = jnp.arange(listed, dtype=jnp.int32)[:, None]
    ranked = []
    for rank in range(2):
        chosen = hits & (later == (rank == 1))
        ranked.append((
            jnp.sum(jnp.where(chosen, table[:, None] + 1, 0), axis=0) - 1,
            jnp.sum(jnp.where(chosen, entries, 0), axis=0),
            jnp.sum(jnp.where(chosen, dest_slot[0][:, None] + 1, 0), axis=0) - 1,
        ))
    slots = lax.all_to_all(jnp.stack([ranked[0][2], ranked[1][2]], axis=1), ("front", "grid"), split_axis=0, concat_axis=0, tiled=True)
    arrived = []
    for rank in range(2):
        tile, entry, _ = ranked[rank]
        moved = tiles(tile, entry, whi, wlo, row_map[0], trailing[0], border_all)
        arrived.append(lax.all_to_all(moved, ("front", "grid"), split_axis=0, concat_axis=0, tiled=True))
    sums = slot_sums(slots[:, 0], arrived[0])
    sums = slot_sums(slots[:, 1], arrived[1], sums)
    return pivot_factor[None], border_factor[None], sums


def solution(mesh):
    return jax.shard_map(
        body,
        mesh=mesh,
        in_specs=(
            P("front", None, None),
            P("front", "grid", None),
            P("front", "grid", None),
            P("front", "grid", None),
            P("front", "grid"),
            P("front", "grid", None),
        ),
        out_specs=(
            P("front", None, None),
            P("front", "grid", None),
            P(("front", "grid"), None, None),
        ),
        check_vma=False,
    )
```

time: 680 us -> 443 us (0.65); the launches traced: 670 us -> 441 us
  Pallas kernels: 0 us -> 140 us
  matrix products: 124 us -> 1.01 us
  other arithmetic: 115 us -> 2.26 us
  local copies, waits for them, and re-layouts: 94 us -> 15.1 us
  waiting for transfers between devices: 291 us -> 232 us
  starting transfers between devices: 20.1 us -> 37.1 us
  loops' own time: 8.6 us -> 0 us
    pallas_call x0 -> x5, Pallas kernels: none -> 140 us  [the longest x2 72.7 us: tiles(): pl.pallas_call(tiles_kernel, out_shape=jax.ShapeDtypeStruct((count, BLK,...]
    dot_general x8 -> x1, matrix products: 119 us -> 1.01 us  [body(): jnp.dot(before.astype(jnp.bfloat16), counted.astype(jnp.bfloat16), prefer...]
    another operation x24 -> x0, other arithmetic: 109 us -> none  [the longest x7 34.6 us: factor_panels(): second_factor = jnp.linalg.cholesky(updated_pivot)]
    all_to_all x2 -> x3, waiting for transfers between devices: 252 us -> 177 us  [the longest x2 177 us: body(): lax.all_to_all(moved, ('front', 'grid'), split_axis=0, concat_axis=0, til...]
    reshape x3 -> x0, local copies, waits for them, and re-layouts: 57.8 us -> none  [the longest x2 38 us: body(): arrived = arrived.reshape(devices * capacity, BLK * BLK)]
    all_to_all x2 -> x3, starting transfers between devices: 20 us -> 37.1 us  [the longest x2 26.3 us: body(): lax.all_to_all(moved, ('front', 'grid'), split_axis=0, concat_axis=0, til...]
    all_gather x2 -> x1, waiting for transfers between devices: 39.6 us -> 54 us  [body(): border_all = lax.all_gather(border[0], 'grid', axis=0, tiled=True)]
    another operation x26 -> x0, local copies, waits for them, and re-layouts: 9.2 us -> none
  transfers between devices with their start and end apart: 4 -> 4, of which waited for: 2 -> 3; matrix products, arithmetic and copies ran while one was open for 32% -> 1% of each run, Pallas kernels for 0% -> 29%
where the time goes in v1:
time: 443 us; the launch traced here: 441 us
  waiting for transfers between devices  232 us (52%)
  Pallas kernels  140 us (32%)
  starting transfers between devices  37.1 us (8%)
  local copies, waits for them, and re-layouts  15.1 us (3%)
  between operations  14.2 us (3%)
    all_to_all x2, waiting for transfers between devices, body(): lax.all_to_all(moved, ('front', 'grid'), split_axis=0, concat_axis=0, til...  177 us
    pallas_call x2, Pallas kernels, tiles(): pl.pallas_call(tiles_kernel, out_shape=jax.ShapeDtypeStruct((count, BLK,...  72.7 us
    all_gather x1, waiting for transfers between devices, body(): border_all = lax.all_gather(border[0], 'grid', axis=0, tiled=True)  54 us
    pallas_call x1, Pallas kernels, factor(): pl.pallas_call(factor_kernel, out_shape=(sq, sq, half, half), in_specs=[V...  44.4 us
    all_to_all x2, starting transfers between devices, body(): lax.all_to_all(moved, ('front', 'grid'), split_axis=0, concat_axis=0, til...  26.3 us
    pallas_call x2, Pallas kernels, slot_sums(): pl.pallas_call(functools.partial(sum_kernel, first), out_shape=jax.ShapeD...  22.7 us
    unnamed x16, local copies, waits for them, and re-layouts  14.2 us
    all_to_all x1, starting transfers between devices, body(): lax.all_to_all(jnp.stack([ranked[0][2], ranked[1][2]], axis=1), ('front',...  10.8 us
  transfers between devices with their start and end apart: 4, of which 3 were waited for; matrix products, arithmetic and copies ran while one was open for 1% of the time, Pallas kernels for 29%

profile of v1, /device:TPU:5, one launch (start us, length us, event | category | flops | bytes accessed | tf_op | source)
XLA Modules:
  0.0 441.2 jit_solution(3920847880202022049)
XLA Ops:
  7.2 0.0 all-gather.3.cloned.1.call-start
  7.2 0.7 all-gather.3.cloned.1.call-update
  7.9 0.7 compare_reduce_fusion
  8.6 0.7 dynamic-slice_add_fusion
  9.3 0.7 broadcast_add_fusion
  10.0 1.0 fusion.2
  11.0 0.1 select_reduce_fusion.2
  11.2 0.7 copy.11
  11.9 10.8 %all-to-all-start = ((s32[128,1,2]{2,1,0:T(1,128)}), s32[128,1,2]{2,1,0:T(1,128)S(1)}, u32[]{:S(2)}, u32[]{:S(2)}) async-start(s32[128,1,2]{2,1,0:T(1,128)} %copy.11), calls=%async_computation | async-start | bytes 131072 | tf_op jit(solution)/shard_map/all_to_all | solution.py:238
  22.8 0.0 copy-start.4
  22.8 1.4 copy-done.4
  24.1 1.3 copy-done.5
  25.5 44.4 %factor.1 = (f32[512,512]{1,0:T(8,128)}, f32[512,512]{1,0:T(8,128)}, bf16[512,512]{1,0:T(8,128)(2,1)S(1)}, bf16[512,512]{1,0:T(8,128)(2,1)S(1)}) custom-call(f32[512,512]{1,0:T(8,128)S(1)} %bitcast.18, f32[512,512]{1,0:T(8,128)S(1)} %bitcast.17), custom_call_target="tpu_custom_call" | custom-call | tf_op jit(solution)/shard_map/factor/pallas_call | solution.py:92
  69.9 54.0 %all-gather.3.cloned.1.call-done = f32[1,8192,512]{2,1,0:T(8,128)} async-done(((f32[1,512,512]{2,1,0:T(8,128)}), f32[1,8192,512]{2,1,0:T(8,128)}) %all-gather.3.cloned.1.call-update) | async-done | bytes 16777232 | tf_op jit(solution)/shard_map/all_gather | solution.py:218
  123.9 0.9 copy-done.6
  124.8 52.0 %tiles.2 = f32[128,128,128]{2,1,0:T(8,128)S(1)} custom-call(s32[128]{0:T(128)S(1)} %broadcast_add_fusion.2.tile_ref, s32[128]{0:T(128)S(1)} %get-tuple-element.16.entry_ref, bf16[512,512]{1,0:T(8,128)(2,1)S(1)} %get-tuple-element.9.whi_ref, bf16[512,512]{1,0:T(8,128)(2,1)S(1)} %get-tuple-element.10.wlo_ref, s32[160,128]{1,0:T(8,128)S(1)} %bitcast.19, ...), custom_call_target="tpu_custom_call" | custom-call | flops 7516192768 | bytes 50331648 | tf_op jit(solution)/shard_map/tiles/pallas_call | solution.py:161
  176.7 0.0 copy-start.1
  176.7 3.2 copy-done.1
  179.9 0.0 all-to-all-done
  179.9 21.3 %all-to-all-start.1 = ((f32[128,128,128]{2,1,0:T(8,128)}), f32[128,128,128]{2,1,0:T(8,128)}, u32[]{:S(2)}, u32[]{:S(2)}) async-start(f32[128,128,128]{2,1,0:T(8,128)} %copy-done.1), calls=%async_computation.1 | async-start | bytes 16777216 | tf_op jit(solution)/shard_map/all_to_all | solution.py:243
  201.2 0.0 copy-done.7
  201.3 20.8 %tiles.3 = f32[128,128,128]{2,1,0:T(8,128)S(1)} custom-call(s32[128]{0:T(128)S(1)} %broadcast_add_fusion.1.tile_ref, s32[128]{0:T(128)S(1)} %get-tuple-element.23.entry_ref, bf16[512,512]{1,0:T(8,128)(2,1)S(1)} %get-tuple-element.9.whi_ref, bf16[512,512]{1,0:T(8,128)(2,1)S(1)} %get-tuple-element.10.wlo_ref, s32[160,128]{1,0:T(8,128)S(1)} %bitcast.20, ...), custom_call_target="tpu_custom_call" | custom-call | flops 7516192768 | bytes 50331648 | tf_op jit(solution)/shard_map/tiles/pallas_call | solution.py:161
  222.0 3.2 copy-done
  225.3 82.8 %all-to-all-done.1.refs_0_ = f32[128,128,128]{2,1,0:T(8,128)} async-done(((f32[128,128,128]{2,1,0:T(8,128)}), f32[128,128,128]{2,1,0:T(8,128)}, u32[]{:S(2)}, u32[]{:S(2)}) %all-to-all-start.1) | async-done | bytes 8388640 | tf_op jit(solution)/shard_map/all_to_all | solution.py:243
  308.1 5.0 %all-to-all-start.2 = ((f32[128,128,128]{2,1,0:T(8,128)}), f32[128,128,128]{2,1,0:T(8,128)}, u32[]{:S(2)}, u32[]{:S(2)}) async-start(f32[128,128,128]{2,1,0:T(8,128)} %copy-done), calls=%async_computation.2 | async-start | bytes 16777216 | tf_op jit(solution)/shard_map/all_to_all | solution.py:243
  313.1 0.2 slice_reduce_fusion
  313.2 10.4 %slot_sums.2.refs_0_ = f32[64,128,128]{2,1,0:T(8,128)S(1)} custom-call(s32[128]{0:T(128)S(1)} %get-tuple-element.11.slot_ref, f32[128,128,128]{2,1,0:T(8,128)} %all-to-all-done.1.refs_0_), custom_call_target="tpu_custom_call" | custom-call | flops 2097152 | bytes 8388608 | tf_op jit(solution)/shard_map/slot_sums/pallas_call | solution.py:202
  323.6 0.0 copy-start.2
  323.7 2.0 copy-done.2
  325.7 94.1 %all-to-all-done.2.refs_1_ = f32[128,128,128]{2,1,0:T(8,128)} async-done(((f32[128,128,128]{2,1,0:T(8,128)}), f32[128,128,128]{2,1,0:T(8,128)}, u32[]{:S(2)}, u32[]{:S(2)}) %all-to-all-start.2) | async-done | bytes 8388640 | tf_op jit(solution)/shard_map/all_to_all | solution.py:243
  419.8 2.2 copy-done.3
  422.0 12.3 %slot_sums.3 = f32[64,128,128]{2,1,0:T(8,128)} custom-call(s32[128]{0:T(128)S(1)} %get-tuple-element.12.slot_ref, f32[64,128,128]{2,1,0:T(8,128)S(1)} %copy-done.3, f32[128,128,128]{2,1,0:T(8,128)} %all-to-all-done.2.refs_1_), custom_call_target="tpu_custom_call" | custom-call | flops 2097152 | bytes 8388608 | tf_op jit(solution)/shard_map/slot_sums/pallas_call | solution.py:202
  (9 shorter events, 0.0 us)
Async XLA Ops:
  7.2 116.7 %all-gather.3.cloned.1.call-start = ((), (), s32[]{:S(2)}) async-start(), calls=%async_computation.3 | async-start | bytes 17825792 | tf_op jit(solution)/shard_map/all_gather | solution.py:218
  11.9 168.0 %all-to-all-start = ((s32[128,1,2]{2,1,0:T(1,128)}), s32[128,1,2]{2,1,0:T(1,128)S(1)}, u32[]{:S(2)}, u32[]{:S(2)}) async-start(s32[128,1,2]{2,1,0:T(1,128)} %copy.11), calls=%async_computation | async-start | bytes 131072 | tf_op jit(solution)/shard_map/all_to_all | solution.py:238
  22.8 1.4 copy-start.4
  24.1 1.3 copy-start.5
  123.9 0.9 copy-start.6
  176.7 3.2 copy-start.1
  179.9 21.3 %copy-start.7 = (s32[1,160,128]{2,1,0:T(8,128)S(1)}, s32[1,160,128]{2,1,0:T(8,128)}, u32[]{:S(2)}) copy-start(s32[1,160,128]{2,1,0:T(8,128)} %param.12) | copy-start | bytes 245764
  179.9 128.1 %all-to-all-start.1 = ((f32[128,128,128]{2,1,0:T(8,128)}), f32[128,128,128]{2,1,0:T(8,128)}, u32[]{:S(2)}, u32[]{:S(2)}) async-start(f32[128,128,128]{2,1,0:T(8,128)} %copy-done.1), calls=%async_computation.1 | async-start | bytes 16777216 | tf_op jit(solution)/shard_map/all_to_all | solution.py:243
  222.0 3.2 copy-start
  308.1 111.7 %all-to-all-start.2 = ((f32[128,128,128]{2,1,0:T(8,128)}), f32[128,128,128]{2,1,0:T(8,128)}, u32[]{:S(2)}, u32[]{:S(2)}) async-start(f32[128,128,128]{2,1,0:T(8,128)} %copy-done), calls=%async_computation.2 | async-start | bytes 16777216 | tf_op jit(solution)/shard_map/all_to_all | solution.py:243
  323.6 2.0 copy-start.2
  419.8 2.2 copy-start.3
Sparse Core Ops, SparseCore 0:
  10.1 113.6 all-gather.2

commit v2 on v1

v2 whole, which is shorter than its diff:
```python
import functools

import jax
import jax.numpy as jnp
import numpy as np
from jax import lax
from jax.experimental import pallas as pl
from jax.experimental.pallas import tpu as pltpu
from jax.sharding import PartitionSpec as P

BLK = 128
SLOTS = 64
N_GRID = 16
SIDE = 4
TILES_DEV = 160
SUM_GROUP = 8
P_SIZE = 512
HI = lax.Precision.HIGHEST
VMEM = pl.BlockSpec(memory_space=pltpu.VMEM)
ANY = pl.BlockSpec(memory_space=pl.ANY)
MESH = pl.DeviceIdType.MESH
HALF = P_SIZE // 2


def tdot(a, b):
    return lax.dot_general(a, b, (((0,), (0,)), ((), ())), precision=HI, preferred_element_type=jnp.float32)


def factor_diagonal(block):
    aug = jnp.concatenate([block, jnp.eye(BLK, dtype=jnp.float32)], axis=1)
    sub = lax.broadcasted_iota(jnp.int32, (8, BLK), 0)
    sub2 = lax.broadcasted_iota(jnp.int32, (8, 2 * BLK), 0)
    done = []
    for panel in range(BLK // 8):
        rows = aug[:8]
        cols = [jnp.broadcast_to(rows[:, 8 * panel + m : 8 * panel + m + 1], (8, BLK)) for m in range(8)]
        for i in range(8):
            inv = lax.rsqrt(jnp.broadcast_to(cols[i][i : i + 1], (8, BLK)))
            mult = jnp.where(sub > i, cols[i] * inv, 0.0)
            inv2 = jnp.concatenate([inv, inv], axis=1)
            mult2 = jnp.concatenate([mult, mult], axis=1)
            top = jnp.broadcast_to(rows[i : i + 1], (8, 2 * BLK)) * inv2
            rows = jnp.where(sub2 == i, top, rows - mult2 * top)
            for m in range(i + 1, 8):
                cols[m] = cols[m] - mult * (jnp.broadcast_to(cols[m][i : i + 1], (8, BLK)) * inv)
        done.append(rows)
        if panel < BLK // 8 - 1:
            left = rows[:, :BLK]
            update = tdot(left, rows)
            aug = aug[8:] - update[8 * (panel + 1) :]
    full = jnp.concatenate(done, axis=0)
    r = lax.broadcasted_iota(jnp.int32, (BLK, BLK), 0)
    c = lax.broadcasted_iota(jnp.int32, (BLK, BLK), 1)
    return jnp.where(r <= c, full[:, :BLK], 0.0), full[:, BLK:]


def front_kernel(
    a_ref, b_ref, t_ref, map_ref,
    pivot_ref, border_ref, out_ref,
    aug_ref, all_ref, left_ref, right_ref, tile_ref, moved_ref,
    send_sem, recv_sem, local_sem, tile_sem, moved_sem,
):
    front, member = lax.axis_index("front"), lax.axis_index("grid")
    place = (member % SIDE, member // SIDE)

    def at(offset):
        return (place[1] + offset[1]) % SIDE * SIDE + (place[0] + offset[0]) % SIDE

    def along(half, first, second):
        return (first, second) if half == 0 else (second, first)

    def piece(half, source, quarter):
        start, size = (half * HALF, HALF) if quarter is None else (half * HALF + quarter * BLK, BLK)
        return all_ref.at[source, pl.ds(start, size)]

    def copy(half, kind, source, quarter, target):
        part = piece(half, source, quarter)
        return pltpu.make_async_remote_copy(
            src_ref=part, dst_ref=part, send_sem=send_sem.at[half, kind], recv_sem=recv_sem.at[half, kind],
            device_id=(front, target), device_id_type=MESH,
        )

    def send(half, kind, first, second, quarter, step):
        copy(half, kind, at(along(half, first, second)), quarter, at(step)).start()

    def arrived(half, kind, first, second, quarter):
        copy(half, kind, at(along(half, first, second)), quarter, member).wait_recv()

    def open_own():
        for half in range(2):
            send(half, 0, 0, 0, None, along(half, 1, 0))
            send(half, 1, 0, 0, None, along(half, 3, 0))
        for half in range(2):
            second_axis(half, 0)

    def second_axis(half, d):
        send(half, 4 + d, d, 0, None, along(half, 0, 1))
        send(half, 8 + d, d, 0, None, along(half, 0, 3))

    def pass_on(half, d):
        arrived(half, 4 + d, d, 3, None)
        send(half, 12 + d, d, 3, 0, along(half, 0, 1))
        arrived(half, 8 + d, d, 1, None)
        send(half, 16 + d, d, 1, 1, along(half, 0, 3))

    def stage_first():
        for half in range(2):
            arrived(half, 0, 3, 0, None)
            send(half, 2, 3, 0, 0, along(half, 1, 0))
            arrived(half, 1, 1, 0, None)
            send(half, 3, 1, 0, 1, along(half, 3, 0))
        for half in range(2):
            second_axis(half, 3)
            second_axis(half, 1)

    def stage_second():
        for half in range(2):
            arrived(half, 2, 2, 0, 0)
            arrived(half, 3, 2, 0, 1)
            second_axis(half, 2)
        for half in range(2):
            pass_on(half, 0)

    def stage_third():
        for half in range(2):
            pass_on(half, 3)
            pass_on(half, 1)

    def stage_fourth():
        for half in range(2):
            pass_on(half, 2)

    barrier = pltpu.get_barrier_semaphore()
    neighbours = [at((1, 0)), at((3, 0)), at((0, 1)), at((0, 3))]
    for target in neighbours:
        pl.semaphore_signal(barrier, inc=1, device_id=(front, target), device_id_type=MESH)
    own = pltpu.make_async_copy(b_ref, all_ref.at[member], local_sem)
    own.start()
    own.wait()
    pl.semaphore_wait(barrier, 4)
    open_own()

    r = lax.broadcasted_iota(jnp.int32, (P_SIZE, P_SIZE), 0)
    c = lax.broadcasted_iota(jnp.int32, (P_SIZE, P_SIZE), 1)
    aug_ref[:, :P_SIZE] = a_ref[...]
    aug_ref[:, P_SIZE:] = jnp.where(r == c, 1.0, 0.0)
    lane = lax.broadcasted_iota(jnp.int32, (BLK, 2 * P_SIZE), 1)

    def step(b, _):
        start = pl.multiple_of(b * BLK, BLK)
        stripe = aug_ref[pl.ds(start, BLK), :]
        diag = aug_ref[pl.ds(start, BLK), pl.ds(start, BLK)]
        upper, inverse = factor_diagonal(diag)
        solved = jnp.dot(inverse, stripe, precision=HI, preferred_element_type=jnp.float32)
        solved = jnp.where(lane >= start, solved, 0.0)
        aug_ref[pl.ds(start, BLK), :] = solved
        aug_ref[pl.ds(start, BLK), pl.ds(start, BLK)] = upper

        def rest(k, _):
            row = pl.multiple_of(k * BLK, BLK)
            left = aug_ref[pl.ds(start, BLK), pl.ds(row, BLK)]
            aug_ref[pl.ds(row, BLK), :] = aug_ref[pl.ds(row, BLK), :] - tdot(left, aug_ref[pl.ds(start, BLK), :])
            return 0

        lax.fori_loop(b + 1, P_SIZE // BLK, rest, 0)
        for when, stage in enumerate((stage_first, stage_second, stage_third, stage_fourth)):
            pl.when(b == when)(stage)
        return 0

    lax.fori_loop(0, P_SIZE // BLK, step, 0)

    def source_of(i):
        u, v = i % SIDE, i // SIDE
        rx = u + u // 2 - 2 * (u // 3)
        ry = v + v // 2 - 2 * (v // 3)
        return at((rx, ry)), rx, ry, u, v

    def tile_copy(i, slot):
        column = pl.multiple_of(source_of(i)[0] * P_SIZE, P_SIZE)
        return pltpu.make_async_copy(t_ref.at[:, pl.ds(column, P_SIZE)], tile_ref.at[slot], tile_sem.at[slot])

    tile_copy(0, 0).start()
    inverse = jnp.where(r >= c, aug_ref[:, P_SIZE:], 0.0)
    pivot_ref[...] = jnp.where(r >= c, aug_ref[:, :P_SIZE].T, 0.0)
    own_rows = all_ref[member]
    solved = lax.dot_general(own_rows, inverse, (((1,), (1,)), ((), ())), precision=HI, preferred_element_type=jnp.float32)
    border_ref[...] = solved
    weights = jnp.dot(solved, inverse, precision=HI, preferred_element_type=jnp.float32)
    high = weights.astype(jnp.bfloat16)
    left_ref[:, :P_SIZE] = high
    left_ref[:, P_SIZE : 2 * P_SIZE] = high
    left_ref[:, 2 * P_SIZE :] = (weights - high.astype(jnp.float32)).astype(jnp.bfloat16)

    def moved_wait(slot):
        pltpu.make_async_copy(moved_ref.at[slot], out_ref.at[pl.ds(0, 10)], moved_sem.at[slot]).wait()

    def source_step(i, _):
        slot = i % 2
        source, rx, ry, u, v = source_of(i)

        @pl.when(i + 1 < N_GRID)
        def _():
            tile_copy(i + 1, 1 - slot).start()

        @pl.when(u == 3)
        def _():
            arrived(1, 12 + ry, ry, 2, 0)
            arrived(1, 16 + ry, ry, 2, 1)

        @pl.when(v == 3)
        def _():
            arrived(0, 12 + rx, rx, 2, 0)
            arrived(0, 16 + rx, rx, 2, 1)

        rows = all_ref[source]
        upper = rows.astype(jnp.bfloat16)
        right_ref[:, :P_SIZE] = upper
        right_ref[:, P_SIZE : 2 * P_SIZE] = (rows - upper.astype(jnp.float32)).astype(jnp.bfloat16)
        right_ref[:, 2 * P_SIZE :] = upper
        tile_copy(i, slot).wait()

        @pl.when(i >= 2)
        def _():
            moved_wait(slot)

        past = (source - member + N_GRID - 1) // N_GRID
        full = source - past * (source - member - 1)
        listed = 100 + 4 * member
        count = 0
        for pair in range(2):
            low = pair * HALF
            product = lax.dot_general(
                left_ref[low:, :], right_ref[low : low + HALF, :], (((1,), (1,)), ((), ())),
                preferred_element_type=jnp.float32,
            )
            tile_ref[slot, low:, low : low + HALF] = tile_ref[slot, low:, low : low + HALF] - product
            for k in range(2 * pair, 4):
                for m in range(2 * pair, min(2 * pair + 1, k) + 1):
                    entry = 8 * k * (k - 1) + k * (member + 1) + source * k + full + m
                    if m == k:
                        entry = entry + past * (listed + k * (N_GRID - 1 - member) + source - member - 1 - entry)
                    value = tile_ref[slot, k * BLK : (k + 1) * BLK, m * BLK : (m + 1) * BLK]
                    first = value.astype(jnp.bfloat16)
                    last = (value - first.astype(jnp.float32)).astype(jnp.bfloat16)
                    wanted = jnp.broadcast_to(map_ref[pl.ds(entry, 1), :], (BLK, BLK))
                    chosen = wanted == lax.broadcasted_iota(jnp.int32, (BLK, BLK), 0)
                    chosen = jnp.where(chosen, 1.0, 0.0).astype(jnp.bfloat16)
                    moved = lax.dot_general(
                        chosen, jnp.concatenate([first, last], axis=1), (((0,), (0,)), ((), ())),
                        preferred_element_type=jnp.float32,
                    )
                    moved_ref[slot, count] = moved[:, :BLK] + moved[:, BLK:]
                    pltpu.make_async_copy(moved_ref.at[slot, count], out_ref.at[entry], moved_sem.at[slot]).start()
                    count += 1
        return 0

    lax.fori_loop(0, N_GRID, source_step, 0)
    moved_wait(0)
    moved_wait(1)
    for half in range(2):
        for kind in range(20):
            quarter = None if kind < 2 or 4 <= kind < 12 else 0
            copy(half, kind, member, quarter, member).wait_send()


def front_tiles(pivot_block, border, trailing, row_map):
    square = jax.ShapeDtypeStruct((P_SIZE, P_SIZE), jnp.float32)
    return pl.pallas_call(
        front_kernel,
        out_shape=(square, square, jax.ShapeDtypeStruct((TILES_DEV, BLK, BLK), jnp.float32)),
        in_specs=[VMEM, ANY, ANY, VMEM],
        out_specs=(VMEM, VMEM, ANY),
        scratch_shapes=[
            pltpu.VMEM((P_SIZE, 2 * P_SIZE), jnp.float32),
            pltpu.VMEM((N_GRID, P_SIZE, P_SIZE), jnp.float32),
            pltpu.VMEM((P_SIZE, 3 * P_SIZE), jnp.bfloat16),
            pltpu.VMEM((P_SIZE, 3 * P_SIZE), jnp.bfloat16),
            pltpu.VMEM((2, P_SIZE, P_SIZE), jnp.float32),
            pltpu.VMEM((2, 10, BLK, BLK), jnp.float32),
            pltpu.SemaphoreType.DMA((2, 20)),
            pltpu.SemaphoreType.DMA((2, 20)),
            pltpu.SemaphoreType.DMA,
            pltpu.SemaphoreType.DMA((2,)),
            pltpu.SemaphoreType.DMA((2,)),
        ],
        compiler_params=pltpu.CompilerParams(collective_id=0, has_side_effects=True, vmem_limit_bytes=52 << 20),
        name="front_tiles",
    )(pivot_block, border, trailing, row_map)


def spread_kernel(owner_ref, rank_ref, tiles_ref, note_ref, out_ref, held_ref, in_sem, out_sem, note_sem):
    chunk = TILES_DEV // 8
    notes = pltpu.make_async_copy(note_ref, out_ref.at[:, pl.ds(2 * BLK, 8)], note_sem)
    notes.start()

    def load(i):
        part = pl.ds(i * chunk, chunk)
        return pltpu.make_async_copy(tiles_ref.at[part], held_ref.at[part], in_sem.at[i])

    for i in range(8):
        load(i).start()
    for i in range(8):
        load(i).wait()
        for j in range(i * chunk, (i + 1) * chunk):
            row = pl.multiple_of(rank_ref[j] * BLK, BLK)
            pltpu.make_async_copy(held_ref.at[j], out_ref.at[owner_ref[j], pl.ds(row, BLK)], out_sem).start()
    pltpu.make_async_copy(tiles_ref, held_ref, out_sem).wait()
    notes.wait()


def spread(owner, rank, tiles, notes):
    devices = notes.shape[0]
    smem = pl.BlockSpec(memory_space=pltpu.SMEM)
    return pl.pallas_call(
        spread_kernel,
        out_shape=jax.ShapeDtypeStruct((devices, 2 * BLK + 8, BLK), jnp.float32),
        in_specs=[smem, smem, ANY, ANY],
        out_specs=ANY,
        scratch_shapes=[
            pltpu.VMEM((TILES_DEV, BLK, BLK), jnp.float32),
            pltpu.SemaphoreType.DMA((8,)),
            pltpu.SemaphoreType.DMA,
            pltpu.SemaphoreType.DMA,
        ],
        compiler_params=pltpu.CompilerParams(vmem_limit_bytes=60 << 20),
        name="spread",
    )(owner, rank, tiles, notes)


def sum_kernel(slot_ref, arrived_ref, out_ref):
    step = pl.program_id(0)

    @pl.when(step == 0)
    def _():
        out_ref[...] = jnp.zeros_like(out_ref)

    for t in range(SUM_GROUP):
        for rank in range(2):
            slot = slot_ref[2 * (step * SUM_GROUP + t) + rank]

            @pl.when(slot >= 0)
            def _(t=t, rank=rank, slot=slot):
                out_ref[slot] = out_ref[slot] + arrived_ref[t, rank * BLK : (rank + 1) * BLK]


def slot_sums(slot, arrived):
    count, rows, _ = arrived.shape
    return pl.pallas_call(
        sum_kernel,
        out_shape=jax.ShapeDtypeStruct((SLOTS, BLK, BLK), jnp.float32),
        grid_spec=pltpu.PrefetchScalarGridSpec(
            num_scalar_prefetch=1,
            grid=(count // SUM_GROUP,),
            in_specs=[pl.BlockSpec((SUM_GROUP, rows, BLK), lambda i, slot_ref: (i, 0, 0))],
            out_specs=pl.BlockSpec((SLOTS, BLK, BLK), lambda i, slot_ref: (0, 0, 0)),
        ),
        compiler_params=pltpu.CompilerParams(vmem_limit_bytes=16 << 20),
        name="slot_sums",
    )(slot, arrived)


def body(pivot_block, border, trailing, dest_owner, dest_slot, row_map):
    member = lax.axis_index("grid")
    devices = lax.axis_size("front") * lax.axis_size("grid")
    listed = dest_owner.shape[1]
    pivot_factor, border_factor, tiles = front_tiles(pivot_block[0], border[0], trailing[0], row_map[0])
    owner = dest_owner[0, :, 0]
    place = jnp.arange(listed, dtype=jnp.int32)
    same = (owner[:, None] == owner[None, :]) & (place[None, :] < place[:, None])
    rank = jnp.any(same, axis=1).astype(jnp.int32)
    slot = jnp.where(place < 100 + 4 * member, dest_slot[0] + 1, 0)
    hits = owner[None, :] == jnp.arange(devices, dtype=jnp.int32)[:, None]
    slots = [
        jnp.sum(jnp.where(hits & (rank == which)[None, :], slot[None, :], 0), axis=1).astype(jnp.float32)
        for which in range(2)
    ]
    lane = lax.broadcasted_iota(jnp.int32, (devices, 8, BLK), 2)
    notes = jnp.where(lane == 0, slots[0][:, None, None], jnp.where(lane == 1, slots[1][:, None, None], 0.0))
    outgoing = spread(owner, rank, tiles, notes)
    arrived = lax.all_to_all(outgoing, ("front", "grid"), split_axis=0, concat_axis=0, tiled=True)
    pivot_factor, border_factor, arrived = lax.optimization_barrier((pivot_factor, border_factor, arrived))
    slot_in = arrived[:, 2 * BLK, :2].astype(jnp.int32).reshape(-1) - 1
    sums = slot_sums(slot_in, arrived)
    return pivot_factor[None], border_factor[None], sums


def solution(mesh):
    return jax.shard_map(
        body,
        mesh=mesh,
        in_specs=(
            P("front", None, None),
            P("front", "grid", None),
            P("front", "grid", None),
            P("front", "grid", None),
            P("front", "grid"),
            P("front", "grid", None),
        ),
        out_specs=(
            P("front", None, None),
            P("front", "grid", None),
            P(("front", "grid"), None, None),
        ),
        check_vma=False,
    )
```

time: 443 us -> 356 us (0.80)
  waiting for transfers between devices: 232 us -> 0 us
  blocking collectives: 0 us -> 203 us
  starting transfers between devices: 37.1 us -> 0 us
  between operations: 14.2 us -> 0.7 us
  Pallas kernels: 140 us -> 130 us
    all_to_all x0 -> x1, blocking collectives: none -> 203 us  [body(): lax.all_to_all(outgoing, ('front', 'grid'), split_axis=0, concat_axis=0,...]
    all_to_all x3 -> x0, waiting for transfers between devices: 177 us -> none  [the longest x2 177 us: body(): lax.all_to_all(moved, ('front', 'grid'), split_axis=0, concat_axis=0, til...]
    all_gather x1 -> x0, waiting for transfers between devices: 54 us -> none  [body(): border_all = lax.all_gather(border[0], 'grid', axis=0, tiled=True)]
    all_to_all x3 -> x0, starting transfers between devices: 37.1 us -> none  [the longest x2 26.3 us: body(): lax.all_to_all(moved, ('front', 'grid'), split_axis=0, concat_axis=0, til...]
    pallas_call x5 -> x3, Pallas kernels: 140 us -> 130 us  [the longest x1 107 us: front_tiles(): pl.pallas_call(front_kernel, out_shape=(square, square, jax.ShapeDtypeStr...]
    unnamed x16 -> x10, local copies, waits for them, and re-layouts: 14.2 us -> 14.6 us
  transfers between devices with their start and end apart: 4 -> 0, of which waited for: 3 -> 0; matrix products, arithmetic and copies ran while one was open for 1% -> 0% of each run, Pallas kernels for 29% -> 0%
where the time goes in v2:
time: 356 us; the launch traced here: 353 us
  blocking collectives  203 us (57%)
  Pallas kernels  130 us (37%)
  local copies, waits for them, and re-layouts  14.8 us (4%)
  other arithmetic  4.4 us (1%)
    all_to_all x1, blocking collectives, body(): lax.all_to_all(outgoing, ('front', 'grid'), split_axis=0, concat_axis=0,...  203 us
    pallas_call x1, Pallas kernels, front_tiles(): pl.pallas_call(front_kernel, out_shape=(square, square, jax.ShapeDtypeStr...  107 us
    pallas_call x1, Pallas kernels, spread(): pl.pallas_call(spread_kernel, out_shape=jax.ShapeDtypeStruct((devices, 2...  17.8 us
    unnamed x10, local copies, waits for them, and re-layouts  14.6 us

profile of v2, /device:TPU:5, one launch (start us, length us, event | category | flops | bytes accessed | tf_op | source)
XLA Modules:
  0.0 353.0 jit_solution(13816214313787634603)
XLA Ops:
  0.6 0.9 fusion.1
  1.6 0.6 broadcast_compare_fusion
  2.2 0.7 compare_select_fusion
  2.8 0.8 select_reduce_fusion.1
  3.7 1.1 select_select_fusion.note_ref
  4.8 0.0 copy-start.2
  4.8 0.9 copy-done.2
  5.7 106.8 %front_tiles.1 = (f32[512,512]{1,0:T(8,128)S(1)}, f32[512,512]{1,0:T(8,128)}, f32[160,128,128]{2,1,0:T(8,128)}) custom-call(f32[512,512]{1,0:T(8,128)} %bitcast.12, f32[512,512]{1,0:T(8,128)} %bitcast.13, f32[512,8192]{1,0:T(8,128)} %bitcast.10, s32[160,128]{1,0:T(8,128)S(1)} %bitcast.9), custom_call_target="tpu_custom_call" | custom-call | tf_op jit(solution)/shard_map/front_tiles/pallas_call | solution.py:268
  112.5 17.8 %spread.1 = f32[128,264,128]{2,1,0:T(8,128)} custom-call(s32[160]{0:T(256)} %bitcast.16, s32[160]{0:T(256)} %get-tuple-element.19.rank_ref, f32[160,128,128]{2,1,0:T(8,128)} %get-tuple-element.11.tiles_ref, f32[128,8,128]{2,1,0:T(8,128)} %select_select_fusion.note_ref), custom_call_target="tpu_custom_call" | custom-call | tf_op jit(solution)/shard_map/spread/pallas_call | solution.py:314
  130.3 0.0 copy-start.3
  130.3 202.8 %all_to_all.5.arrived_ref = f32[128,264,128]{2,1,0:T(8,128)S(1)} all-to-all(f32[128,264,128]{2,1,0:T(8,128)} %spread.1), channel_id=1, replica_groups=mesh['front'=8,'grid'=16] {'front','grid'}, dimensions={0} | all-to-all | bytes 34603008 | tf_op jit(solution)/shard_map/all_to_all | solution.py:380
  333.1 0.2 add_reduce_fusion
  333.3 0.0 copy-start
  333.3 5.9 %copy-done = f32[128,264,128]{2,1,0:T(8,128)} copy-done((f32[128,264,128]{2,1,0:T(8,128)}, f32[128,264,128]{2,1,0:T(8,128)S(1)}, u32[]{:S(2)}) %copy-start) | copy-done | bytes 17301528
  339.2 0.1 sub.7.slot_ref
  339.3 0.0 copy-start.1
  339.3 5.9 %copy-done.1 = f32[128,264,128]{2,1,0:T(8,128)S(1)} copy-done((f32[128,264,128]{2,1,0:T(8,128)S(1)}, f32[128,264,128]{2,1,0:T(8,128)}, u32[]{:S(2)}) %copy-start.1) | copy-done | bytes 17301528
  345.2 5.8 %slot_sums.1 = f32[64,128,128]{2,1,0:T(8,128)} custom-call(s32[256]{0:T(256)S(1)} %sub.7.slot_ref, f32[128,264,128]{2,1,0:T(8,128)S(1)} %copy-done.1), custom_call_target="tpu_custom_call" | custom-call | tf_op jit(solution)/shard_map/slot_sums/pallas_call | solution.py:348
  351.0 1.0 copy.11
  352.0 0.0 copy-done.3
  352.0 1.0 copy.12
  (3 shorter events, 0.0 us)
Async XLA Ops:
  4.8 0.9 copy-start.2
  130.3 221.7 %copy-start.3 = (f32[512,512]{1,0:T(8,128)S(1)}, f32[512,512]{1,0:T(8,128)}, u32[]{:S(2)}) copy-start(f32[512,512]{1,0:T(8,128)} %get-tuple-element.13) | copy-start | bytes 3145732
  333.3 5.9 %copy-start = (f32[128,264,128]{2,1,0:T(8,128)}, f32[128,264,128]{2,1,0:T(8,128)S(1)}, u32[]{:S(2)}) copy-start(f32[128,264,128]{2,1,0:T(8,128)S(1)} %all_to_all.5.arrived_ref) | copy-start | bytes 51904516
  339.3 5.9 %copy-start.1 = (f32[128,264,128]{2,1,0:T(8,128)S(1)}, f32[128,264,128]{2,1,0:T(8,128)}, u32[]{:S(2)}) copy-start(f32[128,264,128]{2,1,0:T(8,128)} %copy-done) | copy-start | bytes 51904516

commit v3 on v2

--- a/solution.py
+++ b/solution.py
@@ -14,6 +14,7 @@
 SIDE = 4
 TILES_DEV = 160
 SUM_GROUP = 8
+SPREAD_GROUP = 8
 P_SIZE = 512
 HI = lax.Precision.HIGHEST
 VMEM = pl.BlockSpec(memory_space=pltpu.VMEM)
@@ -288,75 +289,69 @@
     )(pivot_block, border, trailing, row_map)
 
 
-def spread_kernel(owner_ref, rank_ref, tiles_ref, note_ref, out_ref, held_ref, in_sem, out_sem, note_sem):
-    chunk = TILES_DEV // 8
-    notes = pltpu.make_async_copy(note_ref, out_ref.at[:, pl.ds(2 * BLK, 8)], note_sem)
-    notes.start()
-
-    def load(i):
-        part = pl.ds(i * chunk, chunk)
-        return pltpu.make_async_copy(tiles_ref.at[part], held_ref.at[part], in_sem.at[i])
-
-    for i in range(8):
-        load(i).start()
-    for i in range(8):
-        load(i).wait()
-        for j in range(i * chunk, (i + 1) * chunk):
-            row = pl.multiple_of(rank_ref[j] * BLK, BLK)
-            pltpu.make_async_copy(held_ref.at[j], out_ref.at[owner_ref[j], pl.ds(row, BLK)], out_sem).start()
-    pltpu.make_async_copy(tiles_ref, held_ref, out_sem).wait()
-    notes.wait()
-
-
-def spread(owner, rank, tiles, notes):
+def spread_kernel(entry_ref, tiles_ref, note_ref, out_ref):
+    step = pl.program_id(0)
+    for t in range(SPREAD_GROUP):
+        for rank in range(2):
+            entry = entry_ref[2 * (step * SPREAD_GROUP + t) + rank]
+
+            @pl.when(entry >= 0)
+            def _(t=t, rank=rank, entry=entry):
+                out_ref[t, rank * BLK : (rank + 1) * BLK] = tiles_ref[entry]
+
+        out_ref[t, 2 * BLK :] = note_ref[t]
+
+
+def spread(entry, tiles, notes):
     devices = notes.shape[0]
-    smem = pl.BlockSpec(memory_space=pltpu.SMEM)
     return pl.pallas_call(
         spread_kernel,
         out_shape=jax.ShapeDtypeStruct((devices, 2 * BLK + 8, BLK), jnp.float32),
-        in_specs=[smem, smem, ANY, ANY],
-        out_specs=ANY,
-        scratch_shapes=[
-            pltpu.VMEM((TILES_DEV, BLK, BLK), jnp.float32),
-            pltpu.SemaphoreType.DMA((8,)),
-            pltpu.SemaphoreType.DMA,
-            pltpu.SemaphoreType.DMA,
-        ],
+        grid_spec=pltpu.PrefetchScalarGridSpec(
+            num_scalar_prefetch=1,
+            grid=(devices // SPREAD_GROUP,),
+            in_specs=[
+                pl.BlockSpec((TILES_DEV, BLK, BLK), lambda i, entry_ref: (0, 0, 0), pipeline_mode=pl.Buffered(1)),
+                pl.BlockSpec((SPREAD_GROUP, 8, BLK), lambda i, entry_ref: (i, 0, 0)),
+            ],
+            out_specs=pl.BlockSpec((SPREAD_GROUP, 2 * BLK + 8, BLK), lambda i, entry_ref: (i, 0, 0)),
+        ),
         compiler_params=pltpu.CompilerParams(vmem_limit_bytes=60 << 20),
         name="spread",
-    )(owner, rank, tiles, notes)
-
-
-def sum_kernel(slot_ref, arrived_ref, out_ref):
+    )(entry, tiles, notes)
+
+
+def sum_kernel(whole_ref, arrived_ref, out_ref, note_ref, sem):
     step = pl.program_id(0)
 
     @pl.when(step == 0)
     def _():
+        notes = pltpu.make_async_copy(whole_ref.at[:, pl.ds(2 * BLK, 1)], note_ref, sem)
+        notes.start()
         out_ref[...] = jnp.zeros_like(out_ref)
+        notes.wait()
 
     for t in range(SUM_GROUP):
         for rank in range(2):
-            slot = slot_ref[2 * (step * SUM_GROUP + t) + rank]
+            slot = note_ref[step * SUM_GROUP + t, 0, rank].astype(jnp.int32) - 1
 
             @pl.when(slot >= 0)
             def _(t=t, rank=rank, slot=slot):
                 out_ref[slot] = out_ref[slot] + arrived_ref[t, rank * BLK : (rank + 1) * BLK]
 
 
-def slot_sums(slot, arrived):
+def slot_sums(arrived):
     count, rows, _ = arrived.shape
     return pl.pallas_call(
         sum_kernel,
         out_shape=jax.ShapeDtypeStruct((SLOTS, BLK, BLK), jnp.float32),
-        grid_spec=pltpu.PrefetchScalarGridSpec(
-            num_scalar_prefetch=1,
-            grid=(count // SUM_GROUP,),
-            in_specs=[pl.BlockSpec((SUM_GROUP, rows, BLK), lambda i, slot_ref: (i, 0, 0))],
-            out_specs=pl.BlockSpec((SLOTS, BLK, BLK), lambda i, slot_ref: (0, 0, 0)),
-        ),
+        grid=(count // SUM_GROUP,),
+        in_specs=[ANY, pl.BlockSpec((SUM_GROUP, rows, BLK), lambda i: (i, 0, 0))],
+        out_specs=pl.BlockSpec((SLOTS, BLK, BLK), lambda i: (0, 0, 0)),
+        scratch_shapes=[pltpu.SMEM((count, 1, BLK), jnp.float32), pltpu.SemaphoreType.DMA],
         compiler_params=pltpu.CompilerParams(vmem_limit_bytes=16 << 20),
         name="slot_sums",
-    )(slot, arrived)
+    )(arrived, arrived)
 
 
 def body(pivot_block, border, trailing, dest_owner, dest_slot, row_map):
@@ -370,17 +365,15 @@
     rank = jnp.any(same, axis=1).astype(jnp.int32)
     slot = jnp.where(place < 100 + 4 * member, dest_slot[0] + 1, 0)
     hits = owner[None, :] == jnp.arange(devices, dtype=jnp.int32)[:, None]
-    slots = [
-        jnp.sum(jnp.where(hits & (rank == which)[None, :], slot[None, :], 0), axis=1).astype(jnp.float32)
-        for which in range(2)
-    ]
+    chosen = [hits & (rank == which)[None, :] for which in range(2)]
+    slots = [jnp.sum(jnp.where(c, slot[None, :], 0), axis=1).astype(jnp.float32) for c in chosen]
+    entry = [jnp.sum(jnp.where(c, place[None, :] + 1, 0), axis=1) - 1 for c in chosen]
     lane = lax.broadcasted_iota(jnp.int32, (devices, 8, BLK), 2)
     notes = jnp.where(lane == 0, slots[0][:, None, None], jnp.where(lane == 1, slots[1][:, None, None], 0.0))
-    outgoing = spread(owner, rank, tiles, notes)
+    outgoing = spread(jnp.stack(entry, axis=1).reshape(-1), tiles, notes)
     arrived = lax.all_to_all(outgoing, ("front", "grid"), split_axis=0, concat_axis=0, tiled=True)
     pivot_factor, border_factor, arrived = lax.optimization_barrier((pivot_factor, border_factor, arrived))
-    slot_in = arrived[:, 2 * BLK, :2].astype(jnp.int32).reshape(-1) - 1
-    sums = slot_sums(slot_in, arrived)
+    sums = slot_sums(arrived)
     return pivot_factor[None], border_factor[None], sums
 
 

time: 356 us -> 345 us (0.969)
  local copies, waits for them, and re-layouts: 14.8 us -> 3.65 us
    unnamed x10 -> x6, local copies, waits for them, and re-layouts: 14.6 us -> 2.83 us
where the time goes in v3:
time: 345 us; the launch traced here: 341 us
  blocking collectives  203 us (59%)
  Pallas kernels  130 us (38%)
  other arithmetic  3.66 us (1%)
  local copies, waits for them, and re-layouts  3.65 us (1%)
    all_to_all x1, blocking collectives, body(): lax.all_to_all(outgoing, ('front', 'grid'), split_axis=0, concat_axis=0,...  203 us
    pallas_call x1, Pallas kernels, front_tiles(): pl.pallas_call(front_kernel, out_shape=(square, square, jax.ShapeDtypeStr...  107 us
    pallas_call x1, Pallas kernels, spread(): pl.pallas_call(spread_kernel, out_shape=jax.ShapeDtypeStruct((devices, 2...  15.4 us
    pallas_call x1, Pallas kernels, slot_sums(): pl.pallas_call(sum_kernel, out_shape=jax.ShapeDtypeStruct((SLOTS, BLK, BL...  7.82 us

profile of v3, /device:TPU:5, one launch (start us, length us, event | category | flops | bytes accessed | tf_op | source)
XLA Modules:
  0.0 340.7 jit_solution(1435961900646410079)
XLA Ops:
  0.7 0.9 fusion.1
  1.6 0.7 compare_select_fusion
  2.3 0.9 select_reduce_fusion.3
  3.2 0.1 copy.10
  3.3 0.7 reshape.54.entry_ref
  4.0 1.1 select_select_fusion.note_ref
  5.2 0.0 copy-start
  5.2 0.9 copy-done
  6.1 106.8 %front_tiles.1 = (f32[512,512]{1,0:T(8,128)S(1)}, f32[512,512]{1,0:T(8,128)}, f32[160,128,128]{2,1,0:T(8,128)}) custom-call(f32[512,512]{1,0:T(8,128)} %bitcast.16, f32[512,512]{1,0:T(8,128)} %bitcast.17, f32[512,8192]{1,0:T(8,128)} %bitcast.14, s32[160,128]{1,0:T(8,128)S(1)} %bitcast.13), custom_call_target="tpu_custom_call" | custom-call | tf_op jit(solution)/shard_map/front_tiles/pallas_call | solution.py:269
  112.8 15.4 %spread.1 = f32[128,264,128]{2,1,0:T(8,128)} custom-call(s32[256]{0:T(256)} %reshape.54.entry_ref, f32[160,128,128]{2,1,0:T(8,128)} %get-tuple-element.11.tiles_ref, f32[128,8,128]{2,1,0:T(8,128)} %select_select_fusion.note_ref), custom_call_target="tpu_custom_call" | custom-call | tf_op jit(solution)/shard_map/spread/pallas_call | solution.py:307
  128.2 202.8 %all_to_all.5.whole_ref.arrived_ref = f32[128,264,128]{2,1,0:T(8,128)S(1)} all-to-all(f32[128,264,128]{2,1,0:T(8,128)} %spread.1), channel_id=1, replica_groups=mesh['front'=8,'grid'=16] {'front','grid'}, dimensions={0} | all-to-all | bytes 34603008 | tf_op jit(solution)/shard_map/all_to_all | solution.py:374
  330.9 0.0 copy-start.1
  330.9 7.8 %slot_sums.1 = f32[64,128,128]{2,1,0:T(8,128)} custom-call(f32[128,264,128]{2,1,0:T(8,128)S(1)} %all_to_all.5.whole_ref.arrived_ref, f32[128,264,128]{2,1,0:T(8,128)S(1)} %all_to_all.5.whole_ref.arrived_ref), custom_call_target="tpu_custom_call" | custom-call | tf_op jit(solution)/shard_map/slot_sums/pallas_call | solution.py:345
  338.8 1.0 copy.13
  339.7 0.0 copy-done.1
  339.7 1.0 copy.14
  (7 shorter events, 0.0 us)
Async XLA Ops:
  5.2 0.9 copy-start
  330.9 8.8 %copy-start.1 = (f32[512,512]{1,0:T(8,128)S(1)}, f32[512,512]{1,0:T(8,128)}, u32[]{:S(2)}) copy-start(f32[512,512]{1,0:T(8,128)} %get-tuple-element.13) | copy-start | bytes 3145732

commit v4 on v3

--- a/solution.py
+++ b/solution.py
@@ -25,6 +25,20 @@
 
 def tdot(a, b):
     return lax.dot_general(a, b, (((0,), (0,)), ((), ())), precision=HI, preferred_element_type=jnp.float32)
+
+
+def split3(a):
+    first = a.astype(jnp.bfloat16).astype(jnp.float32)
+    second = (a - first).astype(jnp.bfloat16).astype(jnp.float32)
+    return first, second, a - first - second
+
+
+def outer8(a, b):
+    a1, a2, a3 = split3(a)
+    b1, b2, b3 = split3(b)
+    left = jnp.concatenate([a1, a1, a2, a2, a1, a3], axis=0).astype(jnp.bfloat16)
+    right = jnp.concatenate([b1, b2, b1, b2, b3, b1], axis=0).astype(jnp.bfloat16)
+    return lax.dot_general(left, right, (((0,), (0,)), ((), ())), preferred_element_type=jnp.float32)
 
 
 def factor_diagonal(block):
@@ -47,7 +61,7 @@
         done.append(rows)
         if panel < BLK // 8 - 1:
             left = rows[:, :BLK]
-            update = tdot(left, rows)
+            update = outer8(left, rows)
             aug = aug[8:] - update[8 * (panel + 1) :]
     full = jnp.concatenate(done, axis=0)
     r = lax.broadcasted_iota(jnp.int32, (BLK, BLK), 0)
@@ -164,14 +178,17 @@
             return 0
 
         lax.fori_loop(b + 1, P_SIZE // BLK, rest, 0)
-        for when, stage in enumerate((stage_first, stage_second, stage_third, stage_fourth)):
-            pl.when(b == when)(stage)
+        pl.when(b == 1)(stage_first)
+        pl.when(b == 3)(stage_second)
         return 0
 
     lax.fori_loop(0, P_SIZE // BLK, step, 0)
 
     def source_of(i):
-        u, v = i % SIDE, i // SIDE
+        late = i // 9
+        odd, k = (i - 9) * late % 2, (i - 9) * late // 2
+        u = (1 - late) * (i % 3) + late * (3 - odd * (3 - k))
+        v = (1 - late) * (i // 3) + late * (k + odd * (3 - k))
         rx = u + u // 2 - 2 * (u // 3)
         ry = v + v // 2 - 2 * (v // 3)
         return at((rx, ry)), rx, ry, u, v
@@ -202,6 +219,9 @@
         @pl.when(i + 1 < N_GRID)
         def _():
             tile_copy(i + 1, 1 - slot).start()
+
+        pl.when(i == 2)(stage_third)
+        pl.when(i == 5)(stage_fourth)
 
         @pl.when(u == 3)
         def _():
@@ -289,36 +309,36 @@
     )(pivot_block, border, trailing, row_map)
 
 
-def spread_kernel(entry_ref, tiles_ref, note_ref, out_ref):
+def spread_kernel(entry_ref, slot_ref, tiles_ref, out_ref):
     step = pl.program_id(0)
+    lane = lax.broadcasted_iota(jnp.int32, (8, BLK), 1)
     for t in range(SPREAD_GROUP):
+        at = 2 * (step * SPREAD_GROUP + t)
         for rank in range(2):
-            entry = entry_ref[2 * (step * SPREAD_GROUP + t) + rank]
+            entry = entry_ref[at + rank]
 
             @pl.when(entry >= 0)
             def _(t=t, rank=rank, entry=entry):
                 out_ref[t, rank * BLK : (rank + 1) * BLK] = tiles_ref[entry]
 
-        out_ref[t, 2 * BLK :] = note_ref[t]
-
-
-def spread(entry, tiles, notes):
-    devices = notes.shape[0]
+        note = jnp.where(lane == 0, slot_ref[at], jnp.where(lane == 1, slot_ref[at + 1], 0))
+        out_ref[t, 2 * BLK :] = note.astype(jnp.float32)
+
+
+def spread(entry, slot, tiles):
+    devices = entry.shape[0] // 2
     return pl.pallas_call(
         spread_kernel,
         out_shape=jax.ShapeDtypeStruct((devices, 2 * BLK + 8, BLK), jnp.float32),
         grid_spec=pltpu.PrefetchScalarGridSpec(
-            num_scalar_prefetch=1,
+            num_scalar_prefetch=2,
             grid=(devices // SPREAD_GROUP,),
-            in_specs=[
-                pl.BlockSpec((TILES_DEV, BLK, BLK), lambda i, entry_ref: (0, 0, 0), pipeline_mode=pl.Buffered(1)),
-                pl.BlockSpec((SPREAD_GROUP, 8, BLK), lambda i, entry_ref: (i, 0, 0)),
-            ],
-            out_specs=pl.BlockSpec((SPREAD_GROUP, 2 * BLK + 8, BLK), lambda i, entry_ref: (i, 0, 0)),
+            in_specs=[pl.BlockSpec(memory_space=pltpu.VMEM)],
+            out_specs=pl.BlockSpec((SPREAD_GROUP, 2 * BLK + 8, BLK), lambda i, entry_ref, slot_ref: (i, 0, 0)),
         ),
-        compiler_params=pltpu.CompilerParams(vmem_limit_bytes=60 << 20),
+        compiler_params=pltpu.CompilerParams(vmem_limit_bytes=24 << 20),
         name="spread",
-    )(entry, tiles, notes)
+    )(entry, slot, tiles)
 
 
 def sum_kernel(whole_ref, arrived_ref, out_ref, note_ref, sem):
@@ -366,11 +386,9 @@
     slot = jnp.where(place < 100 + 4 * member, dest_slot[0] + 1, 0)
     hits = owner[None, :] == jnp.arange(devices, dtype=jnp.int32)[:, None]
     chosen = [hits & (rank == which)[None, :] for which in range(2)]
-    slots = [jnp.sum(jnp.where(c, slot[None, :], 0), axis=1).astype(jnp.float32) for c in chosen]
+    slots = [jnp.sum(jnp.where(c, slot[None, :], 0), axis=1) for c in chosen]
     entry = [jnp.sum(jnp.where(c, place[None, :] + 1, 0), axis=1) - 1 for c in chosen]
-    lane = lax.broadcasted_iota(jnp.int32, (devices, 8, BLK), 2)
-    notes = jnp.where(lane == 0, slots[0][:, None, None], jnp.where(lane == 1, slots[1][:, None, None], 0.0))
-    outgoing = spread(jnp.stack(entry, axis=1).reshape(-1), tiles, notes)
+    outgoing = spread(jnp.stack(entry, axis=1).reshape(-1), jnp.stack(slots, axis=1).reshape(-1), tiles)
     arrived = lax.all_to_all(outgoing, ("front", "grid"), split_axis=0, concat_axis=0, tiled=True)
     pivot_factor, border_factor, arrived = lax.optimization_barrier((pivot_factor, border_factor, arrived))
     sums = slot_sums(arrived)

time: 345 us -> 324 us (0.939)
  Pallas kernels: 130 us -> 108 us
  local copies, waits for them, and re-layouts: 3.65 us -> 7.3 us
    pallas_call x1, Pallas kernels: 15.4 us -> 3.44 us  [spread(): pl.pallas_call(spread_kernel, out_shape=jax.ShapeDtypeStruct((devices, 2...]
    pallas_call x1, Pallas kernels: 107 us -> 96.7 us  [front_tiles(): pl.pallas_call(front_kernel, out_shape=(square, square, jax.ShapeDtypeStr...]
    unnamed x6 -> x8, local copies, waits for them, and re-layouts: 2.83 us -> 6.8 us
where the time goes in v4:
time: 324 us; the launch traced here: 321 us
  blocking collectives  203 us (63%)
  Pallas kernels  108 us (33%)
  local copies, waits for them, and re-layouts  7.3 us (2%)
    all_to_all x1, blocking collectives, body(): lax.all_to_all(outgoing, ('front', 'grid'), split_axis=0, concat_axis=0,...  203 us
    pallas_call x1, Pallas kernels, front_tiles(): pl.pallas_call(front_kernel, out_shape=(square, square, jax.ShapeDtypeStr...  96.7 us
    pallas_call x1, Pallas kernels, slot_sums(): pl.pallas_call(sum_kernel, out_shape=jax.ShapeDtypeStruct((SLOTS, BLK, BL...  7.37 us
    unnamed x8, local copies, waits for them, and re-layouts  6.8 us

profile of v4, /device:TPU:5, one launch (start us, length us, event | category | flops | bytes accessed | tf_op | source)
XLA Modules:
  0.0 321.2 jit_solution(17624993113154460091)
XLA Ops:
  0.6 0.9 fusion.1
  1.6 0.7 compare_select_fusion
  2.3 0.9 select_reduce_fusion.3
  3.2 0.1 copy.12
  3.3 0.1 reshape.52.slot_ref
  3.5 0.1 copy.11
  3.6 0.1 reshape.51.entry_ref
  3.7 0.0 copy-start.1
  3.7 0.9 copy-done.1
  4.6 96.7 %front_tiles.1 = (f32[512,512]{1,0:T(8,128)S(1)}, f32[512,512]{1,0:T(8,128)}, f32[160,128,128]{2,1,0:T(8,128)}) custom-call(f32[512,512]{1,0:T(8,128)} %bitcast.18, f32[512,512]{1,0:T(8,128)} %bitcast.19, f32[512,8192]{1,0:T(8,128)} %bitcast.16, s32[160,128]{1,0:T(8,128)S(1)} %bitcast.15), custom_call_target="tpu_custom_call" | custom-call | tf_op jit(solution)/shard_map/front_tiles/pallas_call | solution.py:289
  101.3 0.0 copy-start
  101.4 4.0 %copy-done = f32[160,128,128]{2,1,0:T(8,128)S(1)} copy-done((f32[160,128,128]{2,1,0:T(8,128)S(1)}, f32[160,128,128]{2,1,0:T(8,128)}, u32[]{:S(2)}) %copy-start) | copy-done | bytes 10485784
  105.3 3.4 %spread.1 = f32[128,264,128]{2,1,0:T(8,128)S(1)} custom-call(s32[256]{0:T(256)S(1)} %reshape.51.entry_ref, s32[256]{0:T(256)S(1)} %reshape.52.slot_ref, f32[160,128,128]{2,1,0:T(8,128)S(1)} %copy-done), custom_call_target="tpu_custom_call" | custom-call | tf_op jit(solution)/shard_map/spread/pallas_call | solution.py:330
  108.8 203.1 %all_to_all.5.whole_ref.arrived_ref = f32[128,264,128]{2,1,0:T(8,128)S(1)} all-to-all(f32[128,264,128]{2,1,0:T(8,128)S(1)} %spread.1), channel_id=1, replica_groups=mesh['front'=8,'grid'=16] {'front','grid'}, dimensions={0} | all-to-all | bytes 34603008 | tf_op jit(solution)/shard_map/all_to_all | solution.py:392
  311.9 0.0 copy-start.2
  311.9 7.4 %slot_sums.1 = f32[64,128,128]{2,1,0:T(8,128)} custom-call(f32[128,264,128]{2,1,0:T(8,128)S(1)} %all_to_all.5.whole_ref.arrived_ref, f32[128,264,128]{2,1,0:T(8,128)S(1)} %all_to_all.5.whole_ref.arrived_ref), custom_call_target="tpu_custom_call" | custom-call | tf_op jit(solution)/shard_map/slot_sums/pallas_call | solution.py:365
  319.2 1.0 copy.15
  320.2 0.0 copy-done.2
  320.2 1.0 copy.16
  (5 shorter events, 0.0 us)
Async XLA Ops:
  3.7 0.9 copy-start.1
  101.3 4.0 %copy-start = (f32[160,128,128]{2,1,0:T(8,128)S(1)}, f32[160,128,128]{2,1,0:T(8,128)}, u32[]{:S(2)}) copy-start(f32[160,128,128]{2,1,0:T(8,128)} %get-tuple-element.11.tiles_ref) | copy-start | bytes 31457284
  311.9 8.4 %copy-start.2 = (f32[512,512]{1,0:T(8,128)S(1)}, f32[512,512]{1,0:T(8,128)}, u32[]{:S(2)}) copy-start(f32[512,512]{1,0:T(8,128)} %get-tuple-element.13) | copy-start | bytes 3145732

commit v5 on v4

--- a/solution.py
+++ b/solution.py
@@ -13,8 +13,8 @@
 N_GRID = 16
 SIDE = 4
 TILES_DEV = 160
-SUM_GROUP = 8
-SPREAD_GROUP = 8
+SUM_GROUP = 16
+SPREAD_GROUP = 16
 P_SIZE = 512
 HI = lax.Precision.HIGHEST
 VMEM = pl.BlockSpec(memory_space=pltpu.VMEM)

time: 324 us -> 324 us (level)
  no operation moved by 1% of the time
where the time goes in v5:
time: 324 us; the launch traced here: 321 us
  blocking collectives  203 us (63%)
  Pallas kernels  107 us (33%)
  local copies, waits for them, and re-layouts  7.3 us (2%)
    all_to_all x1, blocking collectives, body(): lax.all_to_all(outgoing, ('front', 'grid'), split_axis=0, concat_axis=0,...  203 us
    pallas_call x1, Pallas kernels, front_tiles(): pl.pallas_call(front_kernel, out_shape=(square, square, jax.ShapeDtypeStr...  96.7 us
    pallas_call x1, Pallas kernels, slot_sums(): pl.pallas_call(sum_kernel, out_shape=jax.ShapeDtypeStruct((SLOTS, BLK, BL...  7.28 us
    unnamed x8, local copies, waits for them, and re-layouts  6.8 us

profile of v5, /device:TPU:5, one launch (start us, length us, event | category | flops | bytes accessed | tf_op | source)
XLA Modules:
  0.0 321.0 jit_solution(13113312446343958216)
XLA Ops:
  0.6 0.9 fusion.1
  1.6 0.7 compare_select_fusion
  2.3 0.9 select_reduce_fusion.3
  3.2 0.1 copy.12
  3.3 0.1 reshape.52.slot_ref
  3.5 0.1 copy.11
  3.6 0.1 reshape.51.entry_ref
  3.7 0.0 copy-start.1
  3.7 0.9 copy-done.1
  4.6 96.7 %front_tiles.1 = (f32[512,512]{1,0:T(8,128)S(1)}, f32[512,512]{1,0:T(8,128)}, f32[160,128,128]{2,1,0:T(8,128)}) custom-call(f32[512,512]{1,0:T(8,128)} %bitcast.18, f32[512,512]{1,0:T(8,128)} %bitcast.19, f32[512,8192]{1,0:T(8,128)} %bitcast.16, s32[160,128]{1,0:T(8,128)S(1)} %bitcast.15), custom_call_target="tpu_custom_call" | custom-call | tf_op jit(solution)/shard_map/front_tiles/pallas_call | solution.py:289
  101.3 0.0 copy-start
  101.4 4.0 %copy-done = f32[160,128,128]{2,1,0:T(8,128)S(1)} copy-done((f32[160,128,128]{2,1,0:T(8,128)S(1)}, f32[160,128,128]{2,1,0:T(8,128)}, u32[]{:S(2)}) %copy-start) | copy-done | bytes 10485784
  105.3 3.3 %spread.1 = f32[128,264,128]{2,1,0:T(8,128)S(1)} custom-call(s32[256]{0:T(256)S(1)} %reshape.51.entry_ref, s32[256]{0:T(256)S(1)} %reshape.52.slot_ref, f32[160,128,128]{2,1,0:T(8,128)S(1)} %copy-done), custom_call_target="tpu_custom_call" | custom-call | tf_op jit(solution)/shard_map/spread/pallas_call | solution.py:330
  108.7 203.1 %all_to_all.5.whole_ref.arrived_ref = f32[128,264,128]{2,1,0:T(8,128)S(1)} all-to-all(f32[128,264,128]{2,1,0:T(8,128)S(1)} %spread.1), channel_id=1, replica_groups=mesh['front'=8,'grid'=16] {'front','grid'}, dimensions={0} | all-to-all | bytes 34603008 | tf_op jit(solution)/shard_map/all_to_all | solution.py:392
  311.8 0.0 copy-start.2
  311.8 7.3 %slot_sums.1 = f32[64,128,128]{2,1,0:T(8,128)} custom-call(f32[128,264,128]{2,1,0:T(8,128)S(1)} %all_to_all.5.whole_ref.arrived_ref, f32[128,264,128]{2,1,0:T(8,128)S(1)} %all_to_all.5.whole_ref.arrived_ref), custom_call_target="tpu_custom_call" | custom-call | tf_op jit(solution)/shard_map/slot_sums/pallas_call | solution.py:365
  319.0 1.0 copy.15
  320.0 0.0 copy-done.2
  320.0 1.0 copy.16
  (5 shorter events, 0.0 us)
Async XLA Ops:
  3.7 0.9 copy-start.1
  101.3 4.0 %copy-start = (f32[160,128,128]{2,1,0:T(8,128)S(1)}, f32[160,128,128]{2,1,0:T(8,128)}, u32[]{:S(2)}) copy-start(f32[160,128,128]{2,1,0:T(8,128)} %get-tuple-element.11.tiles_ref) | copy-start | bytes 31457284
  311.8 8.3 %copy-start.2 = (f32[512,512]{1,0:T(8,128)S(1)}, f32[512,512]{1,0:T(8,128)}, u32[]{:S(2)}) copy-start(f32[512,512]{1,0:T(8,128)} %get-tuple-element.13) | copy-start | bytes 3145732
